TPU v7x, 32 devices: a whole 2x2x4 slice. The times are simulated.
32 devices in a mesh: shot: 4 (over y, x), gx: 2 (over core), gy: 4 (over z).
Axes of the slice: x: 2, y: 2, z: 4, core: 2. Of those that a mesh axis runs over, the one named last changes fastest.
Arguments:
- fwd_now: float32 [8, 32, 128, 256], P('shot', 'gx', 'gy'), may hold values from -6 to 6
- fwd_next: float32 [8, 32, 128, 256], P('shot', 'gx', 'gy'), may hold values from -6 to 6
- adj_now: float32 [8, 32, 128, 256], P('shot', 'gx', 'gy'), may hold values from -6 to 6
- adj_next: float32 [8, 32, 128, 256], P('shot', 'gx', 'gy'), may hold values from -6 to 6
- courant: float32 [32, 128, 256], P('gx', 'gy'), may hold values from 0.15 to 0.45
- wavelet: float32 [8, 128], P('shot'), may hold values from -24 to 24
- traces: float32 [8, 128, 1024], P('shot'), may hold values from -6 to 6
- src_cells: int32 [8], P('shot'), may hold values from 0 to 4095
- rec_cells: int32 [8, 1024], P('shot'), may hold values from 0 to 4095
- step_index: int32 [8], P('shot'), may hold values from 1 to 127
Outputs:
- forward_prior: float32 [8, 32, 128, 256], P('shot', 'gx', 'gy')
- forward_start: float32 [8, 32, 128, 256], P('shot', 'gx', 'gy')
- adjoint_prior: float32 [8, 32, 128, 256], P('shot', 'gx', 'gy')
- adjoint_start: float32 [8, 32, 128, 256], P('shot', 'gx', 'gy')
- gradient: float32 [32, 128, 256], P('gx', 'gy', 'shot')
Inputs may be any that keep to these rules, and one draw needn't show every extreme that they name: `src_cells`: a horizontal cell x * 128 + y of the grid. `rec_cells`: a horizontal cell x * 128 + y of the grid; several receivers may share a cell. `step_index`: a time step k such that the samples k and k - 1 exist (k ≥ 1).
All inputs are finite; a program needn't handle non-finite values.
Results may differ from a plain program's by a relative error of at most 0.0003.
Values sent between devices are 32-bit elements; how exact they have to be, the bound alone decides.
No kernel may reach another device: no remote copies, remote signals or barrier semaphores. Data moves between devices by JAX's collectives and lax.ppermute only.
A program may use at most 64 MiB of HBM per device.

v0:
```python
import jax
import jax.numpy as jnp
from jax import lax
from jax.sharding import PartitionSpec as P

STEPS = 2
SRC_DEPTH = 4
REC_DEPTH = 6


COEFS = (-205.0 / 72.0, 8.0 / 5.0, -1.0 / 5.0, 8.0 / 315.0, -1.0 / 560.0)


def padded_2(block, sides, width):
    for axis, dim in sides:
        count = lax.axis_size(axis)
        forward = [(i, i + 1) for i in range(count - 1)]
        backward = [(target, source) for source, target in forward]
        low = lax.ppermute(
            lax.slice_in_dim(block, block.shape[dim] - width, None, axis=dim), axis, forward
        )
        high = lax.ppermute(lax.slice_in_dim(block, 0, width, axis=dim), axis, backward)
        block = jnp.concatenate([low, block, high], axis=dim)
    return block


def laplace_padded(padded):
    size_x = padded.shape[-3] - 8
    size_y = padded.shape[-2] - 8
    size_z = padded.shape[-1]
    center = padded[..., 4 : 4 + size_x, 4 : 4 + size_y, :]
    widths = [(0, 0)] * (center.ndim - 1) + [(4, 4)]
    deep = jnp.pad(center, widths)
    total = 3.0 * COEFS[0] * center
    for reach in range(1, 5):
        part = (
            padded[..., 4 + reach : 4 + reach + size_x, 4 : 4 + size_y, :]
            + padded[..., 4 - reach : 4 - reach + size_x, 4 : 4 + size_y, :]
        )
        part = (
            part
            + padded[..., 4 : 4 + size_x, 4 + reach : 4 + reach + size_y, :]
            + padded[..., 4 : 4 + size_x, 4 - reach : 4 - reach + size_y, :]
        )
        part = (
            part
            + deep[..., 4 + reach : 4 + reach + size_z]
            + deep[..., 4 - reach : 4 - reach + size_z]
        )
        total = total + COEFS[reach] * part
    return total


def shards(
    fwd_now, fwd_next, adj_now, adj_next, courant, wavelet, traces, src_cells, rec_cells, step_index
):
    shots_here, width_x, width_y, depth = fwd_now.shape
    mass = courant * courant
    anchor_x = lax.axis_index("gx") * width_x
    anchor_y = lax.axis_index("gy") * width_y
    total_y = width_y * lax.axis_size("gy")
    source_x = src_cells // total_y - anchor_x
    source_y = src_cells % total_y - anchor_y
    cells_x = jnp.arange(width_x, dtype=jnp.int32)[None, :, None, None]
    cells_y = jnp.arange(width_y, dtype=jnp.int32)[None, None, :, None]
    cells_z = jnp.arange(depth, dtype=jnp.int32)[None, None, None, :]
    mask = (
        (cells_x == source_x[:, None, None, None])
        & (cells_y == source_y[:, None, None, None])
        & (cells_z == SRC_DEPTH)
    )
    local_x = rec_cells // total_y - anchor_x
    local_y = rec_cells % total_y - anchor_y
    inside = (local_x >= 0) & (local_x < width_x) & (local_y >= 0) & (local_y < width_y)
    shot_rows = jnp.arange(shots_here, dtype=jnp.int32)[:, None]
    slots = ((shot_rows * width_x + local_x) * width_y + local_y) * depth + REC_DEPTH
    volume = shots_here * width_x * width_y * depth
    slots = jnp.where(inside, slots, volume).reshape(-1)
    image = jnp.zeros((width_x, width_y, depth), jnp.float32)
    u_now, u_next, a_now, a_next = (fwd_now, fwd_next, adj_now, adj_next)
    for offset in range(STEPS):
        moment = step_index - offset
        u_padded = padded_2(u_now, (("gx", 1), ("gy", 2)), 4)
        a_padded = padded_2(mass * a_now, (("gx", 1), ("gy", 2)), 4)
        lap_u = laplace_padded(u_padded)
        lap_a = laplace_padded(a_padded)
        term = jnp.sum(a_now * lap_u, axis=0)
        image = image + term
        sample = jnp.take_along_axis(wavelet, moment[:, None], axis=1)[:, :, None, None]
        u_prev = 2.0 * u_now - u_next + mass * (lap_u + jnp.where(mask, sample, 0.0))
        values = jnp.take_along_axis(traces, moment[:, None, None], axis=1)[:, 0, :]
        inject = (
            jnp.zeros((volume,), jnp.float32)
            .at[slots]
            .add(values.reshape(-1), mode="drop")
            .reshape(u_now.shape)
        )
        a_prev = 2.0 * a_now - a_next + lap_a + inject
        u_next, u_now = (u_now, u_prev)
        a_next, a_now = (a_now, a_prev)
    reduced = lax.psum_scatter(image, "shot", scatter_dimension=2, tiled=True)
    share = depth // lax.axis_size("shot")
    speed = lax.dynamic_slice_in_dim(courant, lax.axis_index("shot") * share, share, 2)
    gradient = 2.0 * speed * reduced / (shots_here * lax.axis_size("shot") * STEPS)
    return (u_next, u_now, a_next, a_now, gradient)


def solution(mesh):
    in_specs = (
        P("shot", "gx", "gy", None),
        P("shot", "gx", "gy", None),
        P("shot", "gx", "gy", None),
        P("shot", "gx", "gy", None),
        P("gx", "gy", None),
        P("shot", None),
        P("shot", None, None),
        P("shot"),
        P("shot", None),
        P("shot"),
    )
    out_specs = (
        P("shot", "gx", "gy", None),
        P("shot", "gx", "gy", None),
        P("shot", "gx", "gy", None),
        P("shot", "gx", "gy", None),
        P("gx", "gy", "shot"),
    )
    return jax.shard_map(shards, mesh=mesh, in_specs=in_specs, out_specs=out_specs, check_vma=False)
```

profile of v0, /device:TPU:0, one launch (start us, length us, event | category | flops | bytes accessed | tf_op | source)
XLA Modules:
  0.0 165.0 jit_solution(16471152170158963665)
XLA Ops:
  7.3 1.9 %fusion.159 = (f32[2,4,32,256]{3,2,1,0:T(8,128)S(1)}, f32[2,4,32,256]{3,2,1,0:T(8,128)}) fusion(f32[2,16,32,256]{3,2,1,0:T(8,128)} %param.14), kind=kLoop, calls=%fused_computation.326 | loop fusion | bytes 1048576 | tf_op jit(solution)/shard_map/slice | solution.py:22
  9.2 2.5 %collective-permute-start.1 = (f32[2,4,32,256]{3,2,1,0:T(8,128)}, f32[2,4,32,256]{3,2,1,0:T(8,128)S(1)}, u32[]{:S(2)}, u32[]{:S(2)}) collective-permute-start(f32[2,4,32,256]{3,2,1,0:T(8,128)} %get-tuple-element.36), channel_id=1, source_target_pairs={{0,4},{1,5},{2,6},{3,7},{8,12},{9,13},{10,14},{11,15},{16,20},{17,... | collective-permute-start | bytes 786440 | tf_op jit(solution)/shard_map/ppermute | solution.py:19
  14.4 1.3 gather_fusion
  18.6 1.3 collective-permute-start.2
  19.9 4.9 %collective-permute-start.3 = (f32[2,24,4,256]{3,2,1,0:T(4,128)S(1)}, f32[2,24,4,256]{3,2,1,0:T(4,128)S(1)}, u32[]{:S(2)}, u32[]{:S(2)}) collective-permute-start(f32[2,24,4,256]{3,2,1,0:T(4,128)S(1)} %get-tuple-element.25), channel_id=1, source_target_pairs={{0,1},{1,2},{2,3},{4,5},{5,6},{6,7},{8,9},{9,10},{10,11},{12,13},{... | collective-permute-start | bytes 589832 | tf_op jit(solution)/shard_map/ppermute | solution.py:19
  24.9 3.3 %collective-permute-done.2 = f32[2,24,4,256]{3,2,1,0:T(4,128)S(1)} collective-permute-done((f32[2,24,4,256]{3,2,1,0:T(4,128)S(1)}, f32[2,24,4,256]{3,2,1,0:T(4,128)S(1)}, u32[]{:S(2)}, u32[]{:S(2)}) %collective-permute-start.2) | collective-permute-done | bytes 196640 | tf_op jit(solution)/shard_map/ppermute | solution.py:22
  28.2 1.7 %collective-permute-done.3 = f32[2,24,4,256]{3,2,1,0:T(4,128)S(1)} collective-permute-done((f32[2,24,4,256]{3,2,1,0:T(4,128)S(1)}, f32[2,24,4,256]{3,2,1,0:T(4,128)S(1)}, u32[]{:S(2)}, u32[]{:S(2)}) %collective-permute-start.3) | collective-permute-done | bytes 196640 | tf_op jit(solution)/shard_map/ppermute | solution.py:19
  30.0 4.2 %multiply_reduce_fusion.1 = (f32[16,32,256]{2,1,0:T(8,128)}, f32[2,16,32,256]{3,2,1,0:T(8,128)S(1)}) fusion(f32[2,16,32,256]{3,2,1,0:T(8,128)S(1)} %copy-done.6, f32[2,24,32,256]{3,2,1,0:T(8,128)S(1)} %get-tuple-element.42, f32[2,24,4,256]{3,2,1,0:T(4,128)S(1)} %collective-permute-done.3, f32[2,24,4,256]{3,2,1,0:T(4,128)S(1)} %collective-permute-done.2, ...), kind=kLoop, calls=%fused_computation.249 | loop fusion | flops 10092544 | bytes 14024704 | tf_op jit(solution)/shard_map/reduce_sum | solution.py:87
  36.8 3.8 %collective-permute-start.5 = (f32[2,4,32,256]{3,2,1,0:T(8,128)}, f32[2,4,32,256]{3,2,1,0:T(8,128)}, u32[]{:S(2)}, u32[]{:S(2)}) collective-permute-start(f32[2,4,32,256]{3,2,1,0:T(8,128)} %get-tuple-element.28), channel_id=1, source_target_pairs={{0,4},{1,5},{2,6},{3,7},{8,12},{9,13},{10,14},{11,15},{16,20},{17,... | collective-permute-start | bytes 786440 | tf_op jit(solution)/shard_map/ppermute | solution.py:19
  44.0 4.4 %collective-permute-start.9 = (f32[2,4,32,256]{3,2,1,0:T(8,128)}, f32[2,4,32,256]{3,2,1,0:T(8,128)}, u32[]{:S(2)}, u32[]{:S(2)}) collective-permute-start(f32[2,4,32,256]{3,2,1,0:T(8,128)} %get-tuple-element.30), channel_id=1, source_target_pairs={{0,4},{1,5},{2,6},{3,7},{8,12},{9,13},{10,14},{11,15},{16,20},{17,... | collective-permute-start | bytes 786440 | tf_op jit(solution)/shard_map/ppermute | solution.py:19
  48.5 1.7 %pad_maximum_fusion.19 = (f32[2,24,4,256]{3,2,1,0:T(4,128)}, f32[2,24,4,256]{3,2,1,0:T(4,128)}) fusion(f32[2,4,32,256]{3,2,1,0:T(8,128)S(1)} %collective-permute-done.4, f32[2,16,32,256]{3,2,1,0:T(8,128)S(1)} %get-tuple-element.40, f32[2,4,32,256]{3,2,1,0:T(8,128)} %collective-permute-done.5), kind=kLoop, calls=%fused_computation.265 | loop fusion | flops 196608 | bytes 1966080 | tf_op jit(solution)/shard_map/slice | solution.py:22
  51.5 5.7 %collective-permute-start.7 = (f32[2,24,4,256]{3,2,1,0:T(4,128)}, f32[2,24,4,256]{3,2,1,0:T(4,128)}, u32[]{:S(2)}, u32[]{:S(2)}) collective-permute-start(f32[2,24,4,256]{3,2,1,0:T(4,128)} %get-tuple-element.19), channel_id=1, source_target_pairs={{0,1},{1,2},{2,3},{4,5},{5,6},{6,7},{8,9},{9,10},{10,11},{12,13},{... | collective-permute-start | bytes 589832 | tf_op jit(solution)/shard_map/ppermute | solution.py:19
  57.3 12.2 %scatter_custom_fusion = f32[262144]{0:T(1024)} fusion(s32[2048]{0:T(1024)S(1)} %bitcast.83, f32[2048]{0:T(1024)S(1)} %bitcast.86, f32[]{:T(128)} %constant.56.clone.1), kind=kCustom, calls=%fused_computation.252 | custom fusion | flops 2048 | bytes 1048580 | tf_op jit(solution)/shard_map/scatter-add | solution.py:95
  69.5 2.5 %reshape.171 = f32[2,16,32,256]{3,2,1,0:T(8,128)} reshape(f32[262144]{0:T(1024)} %scatter_custom_fusion) | data formatting | bytes 2097152 | tf_op jit(solution)/shard_map/reshape | solution.py:96
  73.0 1.3 collective-permute-start.10
  74.3 4.6 %collective-permute-start.11 = (f32[2,24,4,256]{3,2,1,0:T(4,128)S(1)}, f32[2,24,4,256]{3,2,1,0:T(4,128)S(1)}, u32[]{:S(2)}, u32[]{:S(2)}) collective-permute-start(f32[2,24,4,256]{3,2,1,0:T(4,128)S(1)} %get-tuple-element.23), channel_id=1, source_target_pairs={{0,1},{1,2},{2,3},{4,5},{5,6},{6,7},{8,9},{9,10},{10,11},{12,13},{... | collective-permute-start | bytes 589832 | tf_op jit(solution)/shard_map/ppermute | solution.py:19
  78.9 1.5 pad_maximum_fusion
  80.6 1.5 collective-permute-done.11
  82.0 1.5 pad_maximum_fusion.1
  83.6 7.2 %multiply_reduce_fusion = (f32[16,32,256]{2,1,0:T(8,128)}, f32[2,16,32,256]{3,2,1,0:T(8,128)S(1)}, f32[2,16,32,256]{3,2,1,0:T(8,128)S(1)}) fusion(f32[2,16,32,256]{3,2,1,0:T(8,128)} %reshape.171, f32[2,24,36,256]{3,2,1,0:T(8,128)S(1)} %get-tuple-element.21, f32[2,24,36,256]{3,2,1,0:T(8,128)S(1)} %get-tuple-element.20, ...), kind=kLoop, calls=%fused_computation.248 | loop fusion | flops 20840448 | bytes 25690112 | tf_op jit(solution)/shard_map/reduce_sum | solution.py:87
  90.9 1.4 broadcast_multiply_fusion
  93.6 3.1 %collective-permute-start.13 = (f32[2,4,32,256]{3,2,1,0:T(8,128)S(1)}, f32[2,4,32,256]{3,2,1,0:T(8,128)S(1)}, u32[]{:S(2)}, u32[]{:S(2)}) collective-permute-start(f32[2,4,32,256]{3,2,1,0:T(8,128)S(1)} %get-tuple-element.27), channel_id=1, source_target_pairs={{0,4},{1,5},{2,6},{3,7},{8,12},{9,13},{10,14},{11,15},{16,20},{17,... | collective-permute-start | bytes 786440 | tf_op jit(solution)/shard_map/ppermute | solution.py:19
  100.6 5.7 %collective-permute-start.15 = (f32[2,24,4,256]{3,2,1,0:T(4,128)}, f32[2,24,4,256]{3,2,1,0:T(4,128)}, u32[]{:S(2)}, u32[]{:S(2)}) collective-permute-start(f32[2,24,4,256]{3,2,1,0:T(4,128)} %get-tuple-element.15), channel_id=1, source_target_pairs={{0,1},{1,2},{2,3},{4,5},{5,6},{6,7},{8,9},{9,10},{10,11},{12,13},{... | collective-permute-start | bytes 589832 | tf_op jit(solution)/shard_map/ppermute | solution.py:19
  106.3 12.2 %scatter_custom_fusion.1 = f32[262144]{0:T(1024)} fusion(s32[2048]{0:T(1024)S(1)} %bitcast.84, f32[2048]{0:T(1024)S(1)} %bitcast.85, f32[]{:T(128)} %constant.56.clone.1), kind=kCustom, calls=%fused_computation.250 | custom fusion | flops 2048 | bytes 1048580 | tf_op jit(solution)/shard_map/scatter-add | solution.py:95
  118.5 1.5 reshape.172
  120.1 2.1 %add.494 = f32[16,32,256]{2,1,0:T(8,128)} add(f32[16,32,256]{2,1,0:T(8,128)} %get-tuple-element.10, f32[16,32,256]{2,1,0:T(8,128)} %get-tuple-element.7) | non-fusion elementwise | flops 131072 | bytes 1572864 | tf_op jit(solution)/shard_map/add | solution.py:88
  122.2 3.5 %copy.39 = f32[16,32,256]{1,0,2:T(8,128)} copy(f32[16,32,256]{2,1,0:T(8,128)} %add.494) | data formatting | bytes 1048576
  125.7 2.9 %reshape.244 = f32[256,512]{1,0:T(8,128)} reshape(f32[256,16,32]{2,1,0:T(8,128)} %bitcast.78) | data formatting | bytes 1048576
  128.7 1.7 %pad_maximum_fusion.2 = (f32[2,24,36,256]{3,2,1,0:T(8,128)S(1)}, f32[2,24,36,256]{3,2,1,0:T(8,128)S(1)}) fusion(f32[2,24,4,256]{3,2,1,0:T(4,128)} %collective-permute-done.14, f32[2,4,32,256]{3,2,1,0:T(8,128)S(1)} %collective-permute-done.12, f32[2,16,32,256]{3,2,1,0:T(8,128)S(1)} %get-tuple-element.37, f32[2,4,32,256]{3,2,1,0:T(8,128)} %copy-done.14, ...), kind=kLoop, calls=%fused_computation.72 | loop fusion | flops 2654208 | bytes 5505024 | tf_op jit(solution)/shard_map/concatenate | solution.py:23
  130.6 3.2 %fusion.16 = f32[2,16,32,256]{3,2,1,0:T(8,128)} fusion(f32[2,16,32,256]{3,2,1,0:T(8,128)S(1)} %reshape.172, f32[2,16,32,256]{3,2,1,0:T(8,128)S(1)} %get-tuple-element.37, f32[2,4,32,256]{3,2,1,0:T(8,128)S(1)} %copy-done.15, f32[2,4,32,256]{3,2,1,0:T(8,128)S(1)} %collective-permute-done.12, f32[2,24,36,256]{3,2,1,0:T(8,128)S(1)} %get-tuple-element.13, ...), kind=kLoop, calls=%fused_computation.110 | loop fusion | flops 10747904 | bytes 14155776 | tf_op jit(solution)/shard_map/add | solution.py:98
  133.7 21.3 %reduce-scatter.4.cloned.1.call-done = f32[64,512]{1,0:T(8,128)} async-done(((f32[256,512]{1,0:T(8,128)}), f32[64,512]{1,0:T(8,128)}) %reduce-scatter.4.cloned.1.call-update) | async-done | bytes 131088
  156.3 1.8 %multiply_multiply_fusion = f32[16,32,64]{2,1,0:T(8,128)} fusion(f32[16,32,64]{2,1,0:T(8,128)S(1)} %copy.40, f32[16,32,256]{2,1,0:T(8,128)} %param.18, s32[]{:T(128)S(6)} %select_n.78), kind=kLoop, calls=%fused_computation.256 | loop fusion | flops 98304 | bytes 393220 | tf_op jit(solution)/shard_map/div | solution.py:104
  (100 shorter events, 20.9 us)
Async XLA Ops:
  7.2 33.6 %copy-start = (f32[2,128,1024]{2,1,0:T(8,128)S(1)}, f32[2,128,1024]{2,1,0:T(8,128)}, u32[]{:S(2)}) copy-start(f32[2,128,1024]{2,1,0:T(8,128)} %param.20) | copy-start | bytes 3145732
  7.2 9.7 %copy-start.19 = (s32[2]{0:T(128)S(1)}, s32[2]{0:T(128)}, u32[]{:S(2)}) copy-start(s32[2]{0:T(128)} %param.23) | copy-start | bytes 28
  7.2 8.5 %copy-start.1 = (f32[2,128]{1,0:T(2,128)S(1)}, f32[2,128]{1,0:T(2,128)}, u32[]{:S(2)}) copy-start(f32[2,128]{1,0:T(2,128)} %param.19) | copy-start | bytes 3076
  7.2 9.1 %copy-start.18 = (s32[2]{0:T(128)S(1)}, s32[2]{0:T(128)}, u32[]{:S(2)}) copy-start(s32[2]{0:T(128)} %param.21) | copy-start | bytes 28
  7.2 9.6 %copy-start.17 = (s32[2,1024]{1,0:T(2,128)S(1)}, s32[2,1024]{1,0:T(2,128)}, u32[]{:S(2)}) copy-start(s32[2,1024]{1,0:T(2,128)} %param.22) | copy-start | bytes 24580
  7.2 9.7 %copy-start.13 = (f32[16,32,256]{2,1,0:T(8,128)S(1)}, f32[16,32,256]{2,1,0:T(8,128)}, u32[]{:S(2)}) copy-start(f32[16,32,256]{2,1,0:T(8,128)} %param.18) | copy-start | bytes 1572868
  7.2 147.8 %reduce-scatter.4.cloned.1.call-start = ((), (), s32[]{:S(2)}) async-start(), calls=%async_computation.1 | async-start | bytes 655360
  9.2 8.9 %copy-start.3 = (f32[2,16,32,256]{3,2,1,0:T(8,128)S(1)}, f32[2,16,32,256]{3,2,1,0:T(8,128)}, u32[]{:S(2)}) copy-start(f32[2,16,32,256]{3,2,1,0:T(8,128)} %param.14) | copy-start | bytes 3145732
  9.2 8.8 %collective-permute-start.1 = (f32[2,4,32,256]{3,2,1,0:T(8,128)}, f32[2,4,32,256]{3,2,1,0:T(8,128)S(1)}, u32[]{:S(2)}, u32[]{:S(2)}) collective-permute-start(f32[2,4,32,256]{3,2,1,0:T(8,128)} %get-tuple-element.36), channel_id=1, source_target_pairs={{0,4},{1,5},{2,6},{3,7},{8,12},{9,13},{10,14},{11,15},{16,20},{17,... | collective-permute-start | bytes 786440 | tf_op jit(solution)/shard_map/ppermute | solution.py:19
  11.7 6.8 %collective-permute-start = (f32[2,4,32,256]{3,2,1,0:T(8,128)S(1)}, f32[2,4,32,256]{3,2,1,0:T(8,128)S(1)}, u32[]{:S(2)}, u32[]{:S(2)}) collective-permute-start(f32[2,4,32,256]{3,2,1,0:T(8,128)S(1)} %get-tuple-element.35), channel_id=1, source_target_pairs={{4,0},{5,1},{6,2},{7,3},{12,8},{13,9},{14,10},{15,11},{20,16},{21,... | collective-permute-start | bytes 786440 | tf_op jit(solution)/shard_map/ppermute | solution.py:22
  18.1 11.9 %copy-start.6 = (f32[2,16,32,256]{3,2,1,0:T(8,128)S(1)}, f32[2,16,32,256]{3,2,1,0:T(8,128)}, u32[]{:S(2)}) copy-start(f32[2,16,32,256]{3,2,1,0:T(8,128)} %param.16) | copy-start | bytes 3145732
  18.6 9.6 %collective-permute-start.2 = (f32[2,24,4,256]{3,2,1,0:T(4,128)S(1)}, f32[2,24,4,256]{3,2,1,0:T(4,128)S(1)}, u32[]{:S(2)}, u32[]{:S(2)}) collective-permute-start(f32[2,24,4,256]{3,2,1,0:T(4,128)S(1)} %get-tuple-element.24), channel_id=1, source_target_pairs={{1,0},{2,1},{3,2},{5,4},{6,5},{7,6},{9,8},{10,9},{11,10},{13,12},{... | collective-permute-start | bytes 589832 | tf_op jit(solution)/shard_map/ppermute | solution.py:22
  19.9 10.0 %collective-permute-start.3 = (f32[2,24,4,256]{3,2,1,0:T(4,128)S(1)}, f32[2,24,4,256]{3,2,1,0:T(4,128)S(1)}, u32[]{:S(2)}, u32[]{:S(2)}) collective-permute-start(f32[2,24,4,256]{3,2,1,0:T(4,128)S(1)} %get-tuple-element.25), channel_id=1, source_target_pairs={{0,1},{1,2},{2,3},{4,5},{5,6},{6,7},{8,9},{9,10},{10,11},{12,13},{... | collective-permute-start | bytes 589832 | tf_op jit(solution)/shard_map/ppermute | solution.py:19
  30.0 4.2 %copy-start.4 = (f32[2,16,32,256]{3,2,1,0:T(8,128)S(1)}, f32[2,16,32,256]{3,2,1,0:T(8,128)}, u32[]{:S(2)}) copy-start(f32[2,16,32,256]{3,2,1,0:T(8,128)} %param.14) | copy-start | bytes 3145732
  30.0 4.2 %copy-start.11 = (f32[16,32,256]{2,1,0:T(8,128)S(1)}, f32[16,32,256]{2,1,0:T(8,128)}, u32[]{:S(2)}) copy-start(f32[16,32,256]{2,1,0:T(8,128)} %mul.143) | copy-start | bytes 1572868
  30.0 4.2 %copy-start.16 = (f32[2,16,32,256]{3,2,1,0:T(8,128)S(1)}, f32[2,16,32,256]{3,2,1,0:T(8,128)}, u32[]{:S(2)}) copy-start(f32[2,16,32,256]{3,2,1,0:T(8,128)} %param.15) | copy-start | bytes 3145732
  34.5 56.3 %copy-start.2 = (f32[2,16,32,256]{3,2,1,0:T(8,128)}, f32[2,16,32,256]{3,2,1,0:T(8,128)S(1)}, u32[]{:S(2)}) copy-start(f32[2,16,32,256]{3,2,1,0:T(8,128)S(1)} %get-tuple-element.40) | copy-start | bytes 3145732
  35.5 13.0 %collective-permute-start.4 = (f32[2,4,32,256]{3,2,1,0:T(8,128)}, f32[2,4,32,256]{3,2,1,0:T(8,128)S(1)}, u32[]{:S(2)}, u32[]{:S(2)}) collective-permute-start(f32[2,4,32,256]{3,2,1,0:T(8,128)} %get-tuple-element.29), channel_id=1, source_target_pairs={{4,0},{5,1},{6,2},{7,3},{12,8},{13,9},{14,10},{15,11},{20,16},{21,... | collective-permute-start | bytes 786440 | tf_op jit(solution)/shard_map/ppermute | solution.py:22
  36.8 11.7 %collective-permute-start.5 = (f32[2,4,32,256]{3,2,1,0:T(8,128)}, f32[2,4,32,256]{3,2,1,0:T(8,128)}, u32[]{:S(2)}, u32[]{:S(2)}) collective-permute-start(f32[2,4,32,256]{3,2,1,0:T(8,128)} %get-tuple-element.28), channel_id=1, source_target_pairs={{0,4},{1,5},{2,6},{3,7},{8,12},{9,13},{10,14},{11,15},{16,20},{17,... | collective-permute-start | bytes 786440 | tf_op jit(solution)/shard_map/ppermute | solution.py:19
  42.7 29.3 %collective-permute-start.8 = (f32[2,4,32,256]{3,2,1,0:T(8,128)}, f32[2,4,32,256]{3,2,1,0:T(8,128)}, u32[]{:S(2)}, u32[]{:S(2)}) collective-permute-start(f32[2,4,32,256]{3,2,1,0:T(8,128)} %get-tuple-element.31), channel_id=1, source_target_pairs={{4,0},{5,1},{6,2},{7,3},{12,8},{13,9},{14,10},{15,11},{20,16},{21,... | collective-permute-start | bytes 786440 | tf_op jit(solution)/shard_map/ppermute | solution.py:22
  44.0 28.0 %collective-permute-start.9 = (f32[2,4,32,256]{3,2,1,0:T(8,128)}, f32[2,4,32,256]{3,2,1,0:T(8,128)}, u32[]{:S(2)}, u32[]{:S(2)}) collective-permute-start(f32[2,4,32,256]{3,2,1,0:T(8,128)} %get-tuple-element.30), channel_id=1, source_target_pairs={{0,4},{1,5},{2,6},{3,7},{8,12},{9,13},{10,14},{11,15},{16,20},{17,... | collective-permute-start | bytes 786440 | tf_op jit(solution)/shard_map/ppermute | solution.py:19
  50.2 28.7 %collective-permute-start.6 = (f32[2,24,4,256]{3,2,1,0:T(4,128)}, f32[2,24,4,256]{3,2,1,0:T(4,128)}, u32[]{:S(2)}, u32[]{:S(2)}) collective-permute-start(f32[2,24,4,256]{3,2,1,0:T(4,128)} %get-tuple-element.18), channel_id=1, source_target_pairs={{1,0},{2,1},{3,2},{5,4},{6,5},{7,6},{9,8},{10,9},{11,10},{13,12},{... | collective-permute-start | bytes 589832 | tf_op jit(solution)/shard_map/ppermute | solution.py:22
  51.5 27.4 %collective-permute-start.7 = (f32[2,24,4,256]{3,2,1,0:T(4,128)}, f32[2,24,4,256]{3,2,1,0:T(4,128)}, u32[]{:S(2)}, u32[]{:S(2)}) collective-permute-start(f32[2,24,4,256]{3,2,1,0:T(4,128)} %get-tuple-element.19), channel_id=1, source_target_pairs={{0,1},{1,2},{2,3},{4,5},{5,6},{6,7},{8,9},{9,10},{10,11},{12,13},{... | collective-permute-start | bytes 589832 | tf_op jit(solution)/shard_map/ppermute | solution.py:19
  73.0 7.6 %collective-permute-start.10 = (f32[2,24,4,256]{3,2,1,0:T(4,128)S(1)}, f32[2,24,4,256]{3,2,1,0:T(4,128)S(1)}, u32[]{:S(2)}, u32[]{:S(2)}) collective-permute-start(f32[2,24,4,256]{3,2,1,0:T(4,128)S(1)} %get-tuple-element.22), channel_id=1, source_target_pairs={{1,0},{2,1},{3,2},{5,4},{6,5},{7,6},{9,8},{10,9},{11,10},{13,12},{... | collective-permute-start | bytes 589832 | tf_op jit(solution)/shard_map/ppermute | solution.py:22
  74.3 7.7 %collective-permute-start.11 = (f32[2,24,4,256]{3,2,1,0:T(4,128)S(1)}, f32[2,24,4,256]{3,2,1,0:T(4,128)S(1)}, u32[]{:S(2)}, u32[]{:S(2)}) collective-permute-start(f32[2,24,4,256]{3,2,1,0:T(4,128)S(1)} %get-tuple-element.23), channel_id=1, source_target_pairs={{0,1},{1,2},{2,3},{4,5},{5,6},{6,7},{8,9},{9,10},{10,11},{12,13},{... | collective-permute-start | bytes 589832 | tf_op jit(solution)/shard_map/ppermute | solution.py:19
  80.4 3.1 %copy-start.7 = (f32[2,16,32,256]{3,2,1,0:T(8,128)S(1)}, f32[2,16,32,256]{3,2,1,0:T(8,128)}, u32[]{:S(2)}) copy-start(f32[2,16,32,256]{3,2,1,0:T(8,128)} %param.16) | copy-start | bytes 3145732
  83.6 7.3 %copy-start.5 = (f32[2,16,32,256]{3,2,1,0:T(8,128)S(1)}, f32[2,16,32,256]{3,2,1,0:T(8,128)}, u32[]{:S(2)}) copy-start(f32[2,16,32,256]{3,2,1,0:T(8,128)} %param.14) | copy-start | bytes 3145732
  83.6 7.3 %copy-start.12 = (f32[16,32,256]{2,1,0:T(8,128)S(1)}, f32[16,32,256]{2,1,0:T(8,128)}, u32[]{:S(2)}) copy-start(f32[16,32,256]{2,1,0:T(8,128)} %mul.143) | copy-start | bytes 1572868
  92.3 4.4 %collective-permute-start.12 = (f32[2,4,32,256]{3,2,1,0:T(8,128)S(1)}, f32[2,4,32,256]{3,2,1,0:T(8,128)S(1)}, u32[]{:S(2)}, u32[]{:S(2)}) collective-permute-start(f32[2,4,32,256]{3,2,1,0:T(8,128)S(1)} %get-tuple-element.26), channel_id=1, source_target_pairs={{4,0},{5,1},{6,2},{7,3},{12,8},{13,9},{14,10},{15,11},{20,16},{21,... | collective-permute-start | bytes 786440 | tf_op jit(solution)/shard_map/ppermute | solution.py:22
  93.6 4.2 %collective-permute-start.13 = (f32[2,4,32,256]{3,2,1,0:T(8,128)S(1)}, f32[2,4,32,256]{3,2,1,0:T(8,128)S(1)}, u32[]{:S(2)}, u32[]{:S(2)}) collective-permute-start(f32[2,4,32,256]{3,2,1,0:T(8,128)S(1)} %get-tuple-element.27), channel_id=1, source_target_pairs={{0,4},{1,5},{2,6},{3,7},{8,12},{9,13},{10,14},{11,15},{16,20},{17,... | collective-permute-start | bytes 786440 | tf_op jit(solution)/shard_map/ppermute | solution.py:19
  99.3 29.4 %collective-permute-start.14 = (f32[2,24,4,256]{3,2,1,0:T(4,128)}, f32[2,24,4,256]{3,2,1,0:T(4,128)}, u32[]{:S(2)}, u32[]{:S(2)}) collective-permute-start(f32[2,24,4,256]{3,2,1,0:T(4,128)} %get-tuple-element.14), channel_id=1, source_target_pairs={{1,0},{2,1},{3,2},{5,4},{6,5},{7,6},{9,8},{10,9},{11,10},{13,12},{... | collective-permute-start | bytes 589832 | tf_op jit(solution)/shard_map/ppermute | solution.py:22
  100.6 28.1 %collective-permute-start.15 = (f32[2,24,4,256]{3,2,1,0:T(4,128)}, f32[2,24,4,256]{3,2,1,0:T(4,128)}, u32[]{:S(2)}, u32[]{:S(2)}) collective-permute-start(f32[2,24,4,256]{3,2,1,0:T(4,128)} %get-tuple-element.15), channel_id=1, source_target_pairs={{0,1},{1,2},{2,3},{4,5},{5,6},{6,7},{8,9},{9,10},{10,11},{12,13},{... | collective-permute-start | bytes 589832 | tf_op jit(solution)/shard_map/ppermute | solution.py:19
  (5 other events, 7.6 us)
Sparse Core Ops, SparseCore 0:
  128.8 26.1 reduce-scatter.3
where the time goes:
time: 166 us; the launch traced here: 165 us
  other arithmetic  56 us (34%)
  starting transfers between devices  45.1 us (27%)
  waiting for transfers between devices  29.1 us (18%)
  local copies, waits for them, and re-layouts  20.3 us (12%)
  between operations  14.5 us (9%)
    ppermute x8, starting transfers between devices, padded_2(): lax.ppermute(lax.slice_in_dim(block, block.shape[dim] - width, None, axis...  34.7 us
    scatter-add x2, other arithmetic, shards(): inject = jnp.zeros((volume,), jnp.float32).at[slots].add(values.reshape(-...  24.5 us
    unnamed x2, waiting for transfers between devices  21.3 us
    reduce_sum x2, other arithmetic, shards(): term = jnp.sum(a_now * lap_u, axis=0)  11.4 us
    ppermute x8, starting transfers between devices, padded_2(): lax.ppermute(lax.slice_in_dim(block, 0, width, axis=dim), axis, backward)  10.3 us
    unnamed x49, local copies, waits for them, and re-layouts  9.2 us
    concatenate x3, other arithmetic, padded_2(): block = jnp.concatenate([low, block, high], axis=dim)  4.74 us
    ppermute x8, waiting for transfers between devices, padded_2(): lax.ppermute(lax.slice_in_dim(block, block.shape[dim] - width, None, axis...  4.33 us
  transfers between devices with their start and end apart: 17, of which 6 were waited for; matrix products, arithmetic and copies ran while one was open for 33% of the time, Pallas kernels for 0%

commit v1 on v0

v1 whole, which is shorter than its diff:
```python
import functools

import jax
import jax.numpy as jnp
from jax import lax
from jax.experimental import pallas as pl
from jax.experimental.pallas import tpu as pltpu
from jax.sharding import PartitionSpec as P

STEPS = 2
SRC_DEPTH = 4
REC_DEPTH = 6
COEFS = (-205.0 / 72.0, 8.0 / 5.0, -1.0 / 5.0, 8.0 / 315.0, -1.0 / 560.0)
F32 = jnp.float32
VMEM = pl.BlockSpec(memory_space=pltpu.VMEM)
SMEM = pl.BlockSpec(memory_space=pltpu.SMEM)
ANY = pl.BlockSpec(memory_space=pl.ANY)


def iota(dim):
    return lax.broadcasted_iota(jnp.int32, (8, 128), dim)


def even_on(axis):
    return lax.axis_index(axis) % 2 == 0


def pair_permutes(axis):
    count = lax.axis_size(axis)
    perms = []
    for first in (0, 1):
        pairs = [(i, i + 1) for i in range(first, count - 1, 2)]
        if pairs:
            perms.append(pairs + [(b, a) for a, b in pairs])
    return perms


def edge_layer(axis, width, turn, k):
    high = even_on(axis) if turn == 0 else jnp.logical_not(even_on(axis))
    return jnp.where(high, width - 1 - k, k)


def halves(depth):
    return [slice(h * 128, h * 128 + 128) for h in range(depth // 128)]


def write_y_sends(sends, s, x, z, u_low, m_low, u_high, m_high):
    sub = iota(0)
    low = jnp.where(sub < 4, u_low, pltpu.roll(m_low, 4, 0))
    high = jnp.where(sub < 4, pltpu.roll(u_high, 4, 0), m_high)
    even = even_on("gy")
    for turn, ref in enumerate(sends):
        pick = even if turn == 0 else jnp.logical_not(even)
        ref[s, x, :, z] = jnp.where(pick, high, low)


def first_sends(turns_x, turns_y, u_hbm, a_hbm, c_hbm, *refs):
    ys, refs = refs[:turns_y], refs[turns_y:]
    xs, refs = refs[:turns_x], refs[turns_x:]
    u_low, u_high, a_low, a_high, c_low, c_high, u_x, a_x, c_x, sems = refs
    shots, width_x, width_y, depth = u_hbm.shape
    copies = []

    def fetch(src, dst):
        copy = pltpu.make_async_copy(src, dst, sems.at[len(copies)])
        copy.start()
        copies.append(copy)

    for src, low, high in ((u_hbm, u_low, u_high), (a_hbm, a_low, a_high)):
        fetch(src.at[:, :, 0:8, :], low)
        fetch(src.at[:, :, width_y - 8 : width_y, :], high)
    fetch(c_hbm.at[:, 0:8, :], c_low)
    fetch(c_hbm.at[:, width_y - 8 : width_y, :], c_high)
    for turn in range(turns_x):
        first = jnp.minimum(
            edge_layer("gx", width_x, turn, 0), edge_layer("gx", width_x, turn, 3)
        )
        fetch(u_hbm.at[:, pl.ds(first, 4)], u_x.at[turn])
        fetch(a_hbm.at[:, pl.ds(first, 4)], a_x.at[turn])
        fetch(c_hbm.at[pl.ds(first, 4)], c_x.at[turn])
    for copy in copies:
        copy.wait()

    def line(x, carry):
        for z in halves(depth):
            mass_low = c_low[x, :, z] * c_low[x, :, z]
            mass_high = c_high[x, :, z] * c_high[x, :, z]
            for s in range(shots):
                write_y_sends(
                    ys,
                    s,
                    x,
                    z,
                    u_low[s, x, :, z],
                    mass_low * a_low[s, x, :, z],
                    u_high[s, x, :, z],
                    mass_high * a_high[s, x, :, z],
                )
        return carry

    lax.fori_loop(0, width_x, line, 0)
    for turn in range(turns_x):
        top = edge_layer("gx", width_x, turn, 0) > 3
        for k in range(4):
            layer = jnp.where(top, 3 - k, k)
            mass = c_x[turn, layer] * c_x[turn, layer]
            for s in range(shots):
                xs[turn][0, s, k] = u_x[turn, s, layer]
                xs[turn][1, s, k] = mass * a_x[turn, s, layer]


def laplace_tile(field, s, x, row):
    lane = iota(1)
    center = [field[s, h, x + 4, pl.ds(row, 8), :] for h in range(2)]
    total = [3.0 * COEFS[0] * c for c in center]
    for r in range(1, 5):
        right = [pltpu.roll(c, r, 1) for c in center]
        left = [pltpu.roll(c, 128 - r, 1) for c in center]
        low, high = lane < r, lane >= 128 - r
        deep = [
            jnp.where(low, 0.0, right[0]) + jnp.where(high, left[1], left[0]),
            jnp.where(low, right[0], right[1]) + jnp.where(high, 0.0, left[1]),
        ]
        for h in range(2):
            part = field[s, h, x + 4 + r, pl.ds(row, 8), :] + field[s, h, x + 4 - r, pl.ds(row, 8), :]
            part = part + field[s, h, x + 4, pl.ds(row + r, 8), :] + field[s, h, x + 4, pl.ds(row - r, 8), :]
            total[h] = total[h] + COEFS[r] * (part + deep[h])
    return center, total


def march(offset, rows_y, step_ref, src_ref, wave_ref, rec_ref, trace_hbm, u, u_old, a, a_old, cour, *refs):
    image_in, refs = (refs[0], refs[1:]) if offset else (None, refs)
    u_out, a_out, image, field_u, field_m, trace, sems = refs
    shots, width_x, width_y, depth = u.shape
    tiles = width_y // 8
    copies = []
    for s in range(shots):
        moment = step_ref[s] - offset
        block = pl.multiple_of((moment // 8) * 8, 8)
        copy = pltpu.make_async_copy(trace_hbm.at[s, pl.ds(block, 8), :], trace.at[s], sems.at[s])
        copy.start()
        copies.append(copy)
    zero = jnp.zeros((8, 128), F32)
    for field in (field_u, field_m):
        for s in range(shots):
            for h in range(2):
                for x in (0, 1, 2, 3, width_x + 4, width_x + 5, width_x + 6, width_x + 7):
                    for t in range(1, tiles + 1):
                        field[s, h, x, 8 * t : 8 * t + 8, :] = zero

    def fill(x, carry):
        for h, z in enumerate(halves(depth)):
            for t in range(tiles):
                row = slice(8 * t, 8 * t + 8)
                mass = cour[x, row, z] * cour[x, row, z]
                for s in range(shots):
                    field_u[s, h, x + 4, 8 * t + 8 : 8 * t + 16, :] = u[s, x, row, z]
                    field_m[s, h, x + 4, 8 * t + 8 : 8 * t + 16, :] = mass * a[s, x, row, z]
            for field in (field_u, field_m):
                for s in range(shots):
                    field[s, h, x + 4, 0:8, :] = zero
                    field[s, h, x + 4, width_y + 8 : width_y + 16, :] = zero
        return carry

    lax.fori_loop(0, width_x, fill, 0)

    def line(x, carry):
        for t in range(tiles):
            row = slice(8 * t, 8 * t + 8)
            mass = [cour[x, row, z] * cour[x, row, z] for z in halves(depth)]
            terms = [image_in[h, x, row, :] if offset else None for h in range(2)]
            for s in range(shots):
                center, lap_u = laplace_tile(field_u, s, x, 8 * t + 8)
                _, lap_a = laplace_tile(field_m, s, x, 8 * t + 8)
                for h, z in enumerate(halves(depth)):
                    a_now = a[s, x, row, z]
                    term = a_now * lap_u[h]
                    terms[h] = term if terms[h] is None else terms[h] + term
                    u_out[s, x, row, z] = 2.0 * center[h] - u_old[s, x, row, z] + mass[h] * lap_u[h]
                    a_out[s, x, row, z] = 2.0 * a_now - a_old[s, x, row, z] + lap_a[h]
            for h in range(2):
                image[h, x, row, :] = terms[h]
        return carry

    lax.fori_loop(0, width_x, line, 0)

    bits = rows_y.bit_length() - 1
    anchor_x = lax.axis_index("gx") * width_x
    anchor_y = lax.axis_index("gy") * width_y
    lane, sub = iota(1), iota(0)
    for s in range(shots):
        moment = step_ref[s] - offset
        place_x = lax.shift_right_logical(src_ref[s], bits) - anchor_x
        place_y = (src_ref[s] & (rows_y - 1)) - anchor_y
        here = (place_x >= 0) & (place_x < width_x) & (place_y >= 0) & (place_y < width_y)

        @pl.when(here)
        def _():
            row = pl.ds(pl.multiple_of((place_y // 8) * 8, 8), 8)
            speed = cour[place_x, row, 0:128]
            hit = (sub == place_y % 8) & (lane == SRC_DEPTH)
            added = jnp.where(hit, speed * speed * wave_ref[s, moment], 0.0)
            u_out[s, place_x, row, 0:128] = u_out[s, place_x, row, 0:128] + added

        copies[s].wait()
        pick = lax.broadcasted_iota(jnp.int32, trace.shape[1:], 0) == moment % 8
        values = jnp.sum(jnp.where(pick, trace[s], 0.0), axis=0, keepdims=True)
        cells = rec_ref[s : s + 1, :]
        count = cells.shape[1]
        cell_x = lax.shift_right_logical(cells, bits) - anchor_x
        cell_y = (cells & (rows_y - 1)) - anchor_y
        hot_x = lax.broadcasted_iota(jnp.int32, (width_x, count), 0) == cell_x
        hot_y = lax.broadcasted_iota(jnp.int32, (width_y, count), 0) == cell_y
        plane = lax.dot_general(
            jnp.where(hot_y, values, 0.0),
            jnp.where(hot_x, 1.0, 0.0),
            (((1,), (1,)), ((), ())),
            precision=lax.Precision.HIGHEST,
            preferred_element_type=F32,
        )
        depth_mask = lax.broadcasted_iota(jnp.int32, (width_y, 128), 1) == REC_DEPTH
        for x in range(width_x):
            added = jnp.where(depth_mask, plane[:, x : x + 1], 0.0)
            a_out[s, x, :, 0:128] = a_out[s, x, :, 0:128] + added


def packed(load, target, x):
    lane = lax.broadcasted_iota(jnp.int32, (16, 128), 1)
    block = load(target // 2, x)
    top, bottom = block[0:16, :], block[16:32, :]
    front = jnp.where(lane < 64, top, pltpu.roll(bottom, 64, 1))
    back = jnp.where(lane < 64, pltpu.roll(top, 64, 1), bottom)
    return jnp.where(target % 2 == 0, front, back)


def edge(turns_x, turns_y, last, *refs):
    hy, refs = refs[:turns_y], refs[turns_y:]
    hx, refs = refs[:turns_x], refs[turns_x:]
    a, cour, u_in, a_in, image_in, u_out, a_out, image, *sends = refs
    shots, width_x, width_y, depth = a.shape
    sub = iota(0)
    even = even_on("gy")

    def keep(x, carry):
        for s in range(shots):
            u_out[s, x] = u_in[s, x]
            a_out[s, x] = a_in[s, x]
        for h in range(2):
            image[h, x] = image_in[h, x]
        return carry

    lax.fori_loop(0, width_x, keep, 0)

    def coef(values):
        out = jnp.zeros((8, 128), F32)
        for j, v in values:
            out = jnp.where(sub == j, v, out)
        return out

    low_coef = [None] + [coef([(j, COEFS[r]) for j in range(4) if j < r]) for r in range(1, 5)]
    high_coef = [None] + [coef([(p, COEFS[r]) for p in range(4, 8) if p >= 8 - r]) for r in range(1, 5)]

    def turned(v, shift):
        return v if shift % 8 == 0 else pltpu.roll(v, shift % 8, 0)

    def rows(x, carry):
        for h, z in enumerate(halves(depth)):
            terms = [image[h, x, 0:8, :], image[h, x, width_y - 8 : width_y, :]]
            for s in range(shots):
                first = hy[0][s, x, :, z]
                second = hy[1][s, x, :, z] if turns_y > 1 else jnp.zeros_like(first)
                below = jnp.where(even, second, first)
                above = jnp.where(even, first, second)
                for side in range(2):
                    row = slice(0, 8) if side == 0 else slice(width_y - 8, width_y)
                    lap_u = lap_a = None
                    for r in range(1, 5):
                        if side == 0:
                            part_u = low_coef[r] * turned(below, r - 4)
                            part_a = low_coef[r] * turned(below, r)
                        else:
                            part_u = high_coef[r] * turned(above, 8 - r)
                            part_a = high_coef[r] * turned(above, 4 - r)
                        lap_u = part_u if lap_u is None else lap_u + part_u
                        lap_a = part_a if lap_a is None else lap_a + part_a
                    mass = cour[x, row, z] * cour[x, row, z]
                    u_out[s, x, row, z] = u_out[s, x, row, z] + mass * lap_u
                    a_out[s, x, row, z] = a_out[s, x, row, z] + lap_a
                    terms[side] = terms[side] + a[s, x, row, z] * lap_u
            image[h, x, 0:8, :] = terms[0]
            image[h, x, width_y - 8 : width_y, :] = terms[1]
        return carry

    lax.fori_loop(0, width_x, rows, 0)
    for turn in range(turns_x):
        for j in range(4):
            x = edge_layer("gx", width_x, turn, j)
            for h, z in enumerate(halves(depth)):
                term = image[h, x]
                for s in range(shots):
                    lap_u = lap_a = None
                    for k in range(4 - j):
                        part_u = COEFS[j + k + 1] * hx[turn][0, s, k, :, z]
                        part_a = COEFS[j + k + 1] * hx[turn][1, s, k, :, z]
                        lap_u = part_u if lap_u is None else lap_u + part_u
                        lap_a = part_a if lap_a is None else lap_a + part_a
                    mass = cour[x, :, z] * cour[x, :, z]
                    u_out[s, x, :, z] = u_out[s, x, :, z] + mass * lap_u
                    a_out[s, x, :, z] = a_out[s, x, :, z] + lap_a
                    term = term + a[s, x, :, z] * lap_u
                image[h, x] = term
    if last:
        me = lax.axis_index("shot")

        def parts(x, carry):
            for k, ref in enumerate(sends):
                ref[x] = packed(lambda h, x: image[h, x], me ^ k, x)
            return carry

        lax.fori_loop(0, width_x, parts, 0)
        return
    ys, xs = sends[:turns_y], sends[turns_y:]

    def outgoing(x, carry):
        for z in halves(depth):
            tile = []
            for row in (slice(0, 8), slice(width_y - 8, width_y)):
                mass = cour[x, row, z] * cour[x, row, z]
                tile.append((row, mass))
            for s in range(shots):
                (low, mass_low), (high, mass_high) = tile
                write_y_sends(
                    ys,
                    s,
                    x,
                    z,
                    u_out[s, x, low, z],
                    mass_low * a_out[s, x, low, z],
                    u_out[s, x, high, z],
                    mass_high * a_out[s, x, high, z],
                )
        return carry

    lax.fori_loop(0, width_x, outgoing, 0)
    for turn in range(turns_x):
        for k in range(4):
            x = edge_layer("gx", width_x, turn, k)
            mass = cour[x] * cour[x]
            for s in range(shots):
                xs[turn][0, s, k] = u_out[s, x]
                xs[turn][1, s, k] = mass * a_out[s, x]


def finish(scale, cour, own, first, second, third, out):
    me = lax.axis_index("shot")

    def line(x, carry):
        speed = packed(lambda h, x: jnp.where(h == 0, cour[x, :, 0:128], cour[x, :, 128:256]), me, x)
        total = own[x] + first[x] + second[x] + third[x]
        value = 2.0 * speed * total / scale
        out[x, 0:16, :] = value[:, 0:64]
        out[x, 16:32, :] = value[:, 64:128]
        return carry

    lax.fori_loop(0, out.shape[0], line, 0)


def call(body, name, outs, scratch, in_specs, args, cost, limit=40 << 20):
    return pl.pallas_call(
        body,
        name=name,
        out_shape=outs,
        in_specs=in_specs,
        out_specs=[VMEM] * len(outs),
        scratch_shapes=scratch,
        compiler_params=pltpu.CompilerParams(vmem_limit_bytes=limit),
        cost_estimate=pl.CostEstimate(flops=cost, bytes_accessed=cost, transcendentals=0),
    )(*args)


def shards(
    fwd_now, fwd_next, adj_now, adj_next, courant, wavelet, traces, src_cells, rec_cells, step_index
):
    shots, width_x, width_y, depth = fwd_now.shape
    groups = lax.axis_size("shot")
    rows_y = width_y * lax.axis_size("gy")
    assert rows_y & (rows_y - 1) == 0 and depth == 256 and groups == 4 and width_y == 32
    perms_x, perms_y = pair_permutes("gx"), pair_permutes("gy")
    turns_x, turns_y = len(perms_x), len(perms_y)

    def shape(*dims):
        return jax.ShapeDtypeStruct(dims, F32)

    y_send, x_send = (shots, width_x, 8, depth), (2, shots, 4, width_y, depth)
    send_shapes = [shape(*y_send)] * turns_y + [shape(*x_send)] * turns_x
    y_rows, x_rows = (shots, width_x, 8, depth), (turns_x, shots, 4, width_y, depth)
    scratch = [pltpu.VMEM(y_rows, F32)] * 4 + [pltpu.VMEM(y_rows[1:], F32)] * 2
    scratch += [pltpu.VMEM(x_rows, F32)] * 2 + [pltpu.VMEM((turns_x, 4, width_y, depth), F32)]
    scratch += [pltpu.SemaphoreType.DMA((6 + 3 * turns_x,))]
    sends = call(
        functools.partial(first_sends, turns_x, turns_y),
        "first_sends",
        send_shapes,
        scratch,
        [ANY] * 3,
        (fwd_now, adj_now, courant),
        1 << 20,
    )
    u_now, u_next, a_now, a_next = fwd_now, fwd_next, adj_now, adj_next
    image = None
    for offset in range(STEPS):
        last = offset == STEPS - 1
        halo_y = [lax.ppermute(s, "gy", p) for s, p in zip(sends[:turns_y], perms_y)]
        halo_x = [lax.ppermute(s, "gx", p) for s, p in zip(sends[turns_y:], perms_x)]
        padded = pltpu.VMEM((shots, 2, width_x + 8, width_y + 16, 128), F32)
        args = (step_index, src_cells, wavelet, rec_cells, traces, u_now, u_next, a_now, a_next, courant)
        args += (image,) if offset else ()
        state = [shape(*fwd_now.shape)] * 2 + [shape(2, width_x, width_y, 128)]
        u_prev, a_prev, image = call(
            functools.partial(march, offset, rows_y),
            f"march_{offset}",
            state,
            [padded, padded, pltpu.VMEM((shots, 8, traces.shape[-1]), F32), pltpu.SemaphoreType.DMA((shots,))],
            [SMEM] * 3 + [VMEM, ANY] + [VMEM] * (len(args) - 5),
            args,
            16 << 20,
        )
        args = (*halo_y, *halo_x, a_now, courant, u_prev, a_prev, image)
        outs = state + ([shape(width_x, 16, 128)] * groups if last else send_shapes)
        u_prev, a_prev, image, *sends = call(
            functools.partial(edge, turns_x, turns_y, last),
            f"edge_{offset}",
            outs,
            [],
            [VMEM] * len(args),
            args,
            2 << 20,
        )
        u_next, u_now = u_now, u_prev
        a_next, a_now = a_now, a_prev
    parts = [sends[0]]
    for k in range(1, groups):
        parts.append(lax.ppermute(sends[k], "shot", [(i, i ^ k) for i in range(groups)]))
    (gradient,) = call(
        functools.partial(finish, float(shots * groups * STEPS)),
        "finish",
        [shape(width_x, width_y, depth // groups)],
        [],
        [VMEM] * 5,
        (courant, *parts),
        1 << 20,
    )
    return (u_next, u_now, a_next, a_now, gradient)


def solution(mesh):
    fields = P("shot", "gx", "gy", None)
    in_specs = (fields,) * 4 + (
        P("gx", "gy", None),
        P("shot", None),
        P("shot", None, None),
        P("shot"),
        P("shot", None),
        P("shot"),
    )
    out_specs = (fields,) * 4 + (P("gx", "gy", "shot"),)
    return jax.shard_map(shards, mesh=mesh, in_specs=in_specs, out_specs=out_specs, check_vma=False)
```

time: 166 us -> 52.4 us (0.32)
  other arithmetic: 56 us -> 0 us
  starting transfers between devices: 45.1 us -> 12.6 us
  Pallas kernels: 0 us -> 25.2 us
  waiting for transfers between devices: 29.1 us -> 6.19 us
  between operations: 14.5 us -> 0.83 us
  local copies, waits for them, and re-layouts: 20.3 us -> 7.18 us
    ppermute x16 -> x9, starting transfers between devices: 45 us -> 12.6 us  [the longest x4 8.39 us: shards(): lax.ppermute(s, 'gy', p)]
    pallas_call x0 -> x6, Pallas kernels: none -> 25.2 us  [call(): pl.pallas_call(body, name=name, out_shape=outs, in_specs=in_specs, out_sp...]
    scatter-add x2 -> x0, other arithmetic: 24.5 us -> none  [shards(): inject = jnp.zeros((volume,), jnp.float32).at[slots].add(values.reshape(-...]
    unnamed x2 -> x0, waiting for transfers between devices: 21.3 us -> none
    reduce_sum x2 -> x0, other arithmetic: 11.4 us -> none  [shards(): term = jnp.sum(a_now * lap_u, axis=0)]
    add x2 -> x0, other arithmetic: 5.25 us -> none  [the longest x1 3.18 us: shards(): a_prev = 2.0 * a_now - a_next + lap_a + inject]
    concatenate x3 -> x0, other arithmetic: 4.74 us -> none  [padded_2(): block = jnp.concatenate([low, block, high], axis=dim)]
    reshape x2 -> x0, local copies, waits for them, and re-layouts: 4.02 us -> none  [shards(): inject = jnp.zeros((volume,), jnp.float32).at[slots].add(values.reshape(-...]
  transfers between devices with their start and end apart: 17 -> 9, of which waited for: 6 -> 2; matrix products, arithmetic and copies ran while one was open for 33% -> 0% of each run, Pallas kernels for 0% -> 29%
where the time goes in v1:
time: 52.4 us; the launch traced here: 52 us
  Pallas kernels  25.2 us (48%)
  starting transfers between devices  12.6 us (24%)
  local copies, waits for them, and re-layouts  7.18 us (14%)
  waiting for transfers between devices  6.19 us (12%)
  between operations  0.83 us (2%)
    pallas_call x6, Pallas kernels, call(): pl.pallas_call(body, name=name, out_shape=outs, in_specs=in_specs, out_sp...  25.2 us
    ppermute x4, starting transfers between devices, shards(): lax.ppermute(s, 'gy', p)  8.39 us
    unnamed x30, local copies, waits for them, and re-layouts  7.18 us
    ppermute x3, waiting for transfers between devices, shards(): lax.ppermute(sends[k], 'shot', [(i, i ^ k) for i in range(groups)])  6.17 us
    ppermute x3, starting transfers between devices, shards(): lax.ppermute(sends[k], 'shot', [(i, i ^ k) for i in range(groups)])  3.49 us
  transfers between devices with their start and end apart: 9, of which 2 were waited for; matrix products, arithmetic and copies ran while one was open for 0% of the time, Pallas kernels for 29%

profile of v1, /device:TPU:0, one launch (start us, length us, event | category | flops | bytes accessed | tf_op | source)
XLA Modules:
  0.0 52.0 jit_solution(16609423547261363979)
XLA Ops:
  0.6 0.0 copy-start
  0.6 1.0 %copy-done = f32[16,32,256]{2,1,0:T(8,128)S(1)} copy-done((f32[16,32,256]{2,1,0:T(8,128)S(1)}, f32[16,32,256]{2,1,0:T(8,128)}, u32[]{:S(2)}) %copy-start) | copy-done | bytes 524312
  1.7 1.2 %copy-done.2 = f32[2,16,32,256]{3,2,1,0:T(8,128)S(1)} copy-done((f32[2,16,32,256]{3,2,1,0:T(8,128)S(1)}, f32[2,16,32,256]{3,2,1,0:T(8,128)}, u32[]{:S(2)}) %copy-start.2) | copy-done | bytes 1048600
  2.9 1.2 %copy-done.4 = f32[2,16,32,256]{3,2,1,0:T(8,128)S(1)} copy-done((f32[2,16,32,256]{3,2,1,0:T(8,128)S(1)}, f32[2,16,32,256]{3,2,1,0:T(8,128)}, u32[]{:S(2)}) %copy-start.4) | copy-done | bytes 1048600
  4.1 0.6 %first_sends.1 = (f32[2,16,8,256]{3,2,1,0:T(8,128)S(1)}, f32[2,16,8,256]{3,2,1,0:T(8,128)S(1)}, f32[2,2,4,32,256]{4,3,2,1,0:T(8,128)S(1)}) custom-call(f32[2,16,32,256]{3,2,1,0:T(8,128)S(1)} %copy-done.4, f32[2,16,32,256]{3,2,1,0:T(8,128)S(1)} %copy-done.2, f32[16,32,256]{2,1,0:T(8,128)S(1)} %copy-done), custom_call_target="tpu_custom_call" | custom-call | flops 1048576 | bytes 1048576 | tf_op jit(solution)/shard_map/first_sends/pallas_call | solution.py:369
  4.8 0.6 %collective-permute-start.2 = (f32[2,2,4,32,256]{4,3,2,1,0:T(8,128)S(1)}, f32[2,2,4,32,256]{4,3,2,1,0:T(8,128)S(1)}, u32[]{:S(2)}, u32[]{:S(2)}) collective-permute-start(f32[2,2,4,32,256]{4,3,2,1,0:T(8,128)S(1)} %get-tuple-element.28), channel_id=1, source_target_pairs={{0,4},{4,0},{1,5},{5,1},{2,6},{6,2},{3,7},{7,3},{8,12},{12,8},{9,1... | collective-permute-start | bytes 1572872 | tf_op jit(solution)/shard_map/ppermute | solution.py:414
  5.4 2.7 %collective-permute-start = (f32[2,16,8,256]{3,2,1,0:T(8,128)S(1)}, f32[2,16,8,256]{3,2,1,0:T(8,128)S(1)}, u32[]{:S(2)}, u32[]{:S(2)}) collective-permute-start(f32[2,16,8,256]{3,2,1,0:T(8,128)S(1)} %get-tuple-element.26), channel_id=1, source_target_pairs={{0,1},{2,3},{1,0},{3,2},{4,5},{6,7},{5,4},{7,6},{8,9},{10,11},{9,8... | collective-permute-start | bytes 786440 | tf_op jit(solution)/shard_map/ppermute | solution.py:413
  8.0 0.8 %collective-permute-start.1 = (f32[2,16,8,256]{3,2,1,0:T(8,128)S(1)}, f32[2,16,8,256]{3,2,1,0:T(8,128)S(1)}, u32[]{:S(2)}, u32[]{:S(2)}) collective-permute-start(f32[2,16,8,256]{3,2,1,0:T(8,128)S(1)} %get-tuple-element.27), channel_id=1, source_target_pairs={{1,2},{2,1},{5,6},{6,5},{9,10},{10,9},{13,14},{14,13},{17,18},{18,... | collective-permute-start | bytes 786440 | tf_op jit(solution)/shard_map/ppermute | solution.py:413
  8.9 0.0 copy-start.9
  8.9 1.2 %copy-done.9 = f32[2,16,32,256]{3,2,1,0:T(8,128)S(1)} copy-done((f32[2,16,32,256]{3,2,1,0:T(8,128)S(1)}, f32[2,16,32,256]{3,2,1,0:T(8,128)}, u32[]{:S(2)}) %copy-start.9) | copy-done | bytes 1048600
  10.1 7.6 %march_0.1 = (f32[2,16,32,256]{3,2,1,0:T(8,128)S(1)}, f32[2,16,32,256]{3,2,1,0:T(8,128)S(1)}, f32[2,16,32,128]{3,2,1,0:T(8,128)S(1)}) custom-call(s32[2]{0:T(128)S(1)} %copy-done.13, s32[2]{0:T(128)S(1)} %copy-done.14, f32[2,128]{1,0:T(2,128)S(1)} %copy-done.12, s32[2,1024]{1,0:T(2,128)S(1)} %copy-done.11, f32[2,128,1024]{2,1,0:T(8,128)S(1)} %copy-done.7, ...), custom_call_target="tpu_custom_call" | custom-call | flops 16777216 | bytes 16777216 | tf_op jit(solution)/shard_map/march_0/pallas_call | solution.py:369
  17.7 0.0 collective-permute-done.refs_0_
  17.7 0.0 collective-permute-done.1.refs_1_
  17.7 0.0 collective-permute-done.2.refs_2_
  17.8 2.4 %edge_0.1 = (f32[2,16,32,256]{3,2,1,0:T(8,128)}, f32[2,16,32,256]{3,2,1,0:T(8,128)}, f32[2,16,32,128]{3,2,1,0:T(8,128)S(1)}, f32[2,16,8,256]{3,2,1,0:T(8,128)S(1...) custom-call(f32[2,16,8,256]{3,2,1,0:T(8,128)S(1)} %collective-permute-done.refs_0_, ...), custom_call_target="tpu_custom_call" | custom-call | flops 2097152 | bytes 2097152 | tf_op jit(solution)/shard_map/edge_0/pallas_call | solution.py:369
  20.2 0.1 collective-permute-start.5
  20.3 4.3 %collective-permute-start.3 = (f32[2,16,8,256]{3,2,1,0:T(8,128)S(1)}, f32[2,16,8,256]{3,2,1,0:T(8,128)S(1)}, u32[]{:S(2)}, u32[]{:S(2)}) collective-permute-start(f32[2,16,8,256]{3,2,1,0:T(8,128)S(1)} %get-tuple-element.33), channel_id=1, source_target_pairs={{0,1},{2,3},{1,0},{3,2},{4,5},{6,7},{5,4},{7,6},{8,9},{10,11},{9,8... | collective-permute-start | bytes 786440 | tf_op jit(solution)/shard_map/ppermute | solution.py:413
  24.6 0.7 %collective-permute-start.4 = (f32[2,16,8,256]{3,2,1,0:T(8,128)S(1)}, f32[2,16,8,256]{3,2,1,0:T(8,128)S(1)}, u32[]{:S(2)}, u32[]{:S(2)}) collective-permute-start(f32[2,16,8,256]{3,2,1,0:T(8,128)S(1)} %get-tuple-element.34), channel_id=1, source_target_pairs={{1,2},{2,1},{5,6},{6,5},{9,10},{10,9},{13,14},{14,13},{17,18},{18,... | collective-permute-start | bytes 786440 | tf_op jit(solution)/shard_map/ppermute | solution.py:413
  25.2 0.0 copy-start.5
  25.3 1.2 %copy-done.5 = f32[2,16,32,256]{3,2,1,0:T(8,128)S(1)} copy-done((f32[2,16,32,256]{3,2,1,0:T(8,128)S(1)}, f32[2,16,32,256]{3,2,1,0:T(8,128)}, u32[]{:S(2)}) %copy-start.5) | copy-done | bytes 1048600
  26.5 1.2 %copy-done.10 = f32[2,16,32,256]{3,2,1,0:T(8,128)S(1)} copy-done((f32[2,16,32,256]{3,2,1,0:T(8,128)S(1)}, f32[2,16,32,256]{3,2,1,0:T(8,128)}, u32[]{:S(2)}) %copy-start.10) | copy-done | bytes 1048600
  27.7 7.7 %march_1.1 = (f32[2,16,32,256]{3,2,1,0:T(8,128)S(1)}, f32[2,16,32,256]{3,2,1,0:T(8,128)S(1)}, f32[2,16,32,128]{3,2,1,0:T(8,128)S(1)}) custom-call(s32[2]{0:T(128)S(1)} %copy-done.13, s32[2]{0:T(128)S(1)} %copy-done.14, f32[2,128]{1,0:T(2,128)S(1)} %copy-done.12, s32[2,1024]{1,0:T(2,128)S(1)} %copy-done.11, f32[2,128,1024]{2,1,0:T(8,128)S(1)} %copy-done.7, ...), custom_call_target="tpu_custom_call" | custom-call | flops 16777216 | bytes 16777216 | tf_op jit(solution)/shard_map/march_1/pallas_call | solution.py:369
  35.4 0.0 collective-permute-done.3.refs_0_
  35.4 0.0 collective-permute-done.4.refs_1_
  35.4 3.8 %edge_1.1 = (f32[2,16,32,256]{3,2,1,0:T(8,128)}, f32[2,16,32,256]{3,2,1,0:T(8,128)}, f32[2,16,32,128]{3,2,1,0:T(8,128)}, f32[16,16,128]{2,1,0:T(8,128)S(1)}, f32...) custom-call(f32[2,16,8,256]{3,2,1,0:T(8,128)S(1)} %collective-permute-done.3.refs_0_, ...), custom_call_target="tpu_custom_call" | custom-call | flops 2097152 | bytes 2097152 | tf_op jit(solution)/shard_map/edge_1/pallas_call | solution.py:369
  39.2 1.5 %collective-permute-start.6 = (f32[16,16,128]{2,1,0:T(8,128)S(1)}, f32[16,16,128]{2,1,0:T(8,128)S(1)}, u32[]{:S(2)}, u32[]{:S(2)}) collective-permute-start(f32[16,16,128]{2,1,0:T(8,128)S(1)} %get-tuple-element.44), channel_id=1, source_target_pairs={{0,8},{8,0},{16,24},{24,16},{1,9},{9,1},{17,25},{25,17},{2,10},{10... | collective-permute-start | bytes 393224 | tf_op jit(solution)/shard_map/ppermute | solution.py:443
  40.7 1.5 %collective-permute-start.7 = (f32[16,16,128]{2,1,0:T(8,128)S(1)}, f32[16,16,128]{2,1,0:T(8,128)S(1)}, u32[]{:S(2)}, u32[]{:S(2)}) collective-permute-start(f32[16,16,128]{2,1,0:T(8,128)S(1)} %get-tuple-element.45), channel_id=1, source_target_pairs={{0,16},{8,24},{16,0},{24,8},{1,17},{9,25},{17,1},{25,9},{2,18},{10... | collective-permute-start | bytes 393224 | tf_op jit(solution)/shard_map/ppermute | solution.py:443
  42.2 0.5 collective-permute-start.8
  42.7 2.6 %collective-permute-done.6.first = f32[16,16,128]{2,1,0:T(8,128)S(1)} collective-permute-done((f32[16,16,128]{2,1,0:T(8,128)S(1)}, f32[16,16,128]{2,1,0:T(8,128)S(1)}, u32[]{:S(2)}, u32[]{:S(2)}) %collective-permute-start.6) | collective-permute-done | bytes 131104 | tf_op jit(solution)/shard_map/ppermute | solution.py:443
  45.3 3.6 %collective-permute-done.7.second = f32[16,16,128]{2,1,0:T(8,128)S(1)} collective-permute-done((f32[16,16,128]{2,1,0:T(8,128)S(1)}, f32[16,16,128]{2,1,0:T(8,128)S(1)}, u32[]{:S(2)}, u32[]{:S(2)}) %collective-permute-start.7) | collective-permute-done | bytes 131104 | tf_op jit(solution)/shard_map/ppermute | solution.py:443
  48.9 0.0 collective-permute-done.8.third
  48.9 3.1 %finish.1 = f32[16,32,64]{2,1,0:T(8,128)} custom-call(f32[16,32,256]{2,1,0:T(8,128)S(1)} %copy-done.1, f32[16,16,128]{2,1,0:T(8,128)S(1)} %get-tuple-element.43.own, f32[16,16,128]{2,1,0:T(8,128)S(1)} %collective-permute-done.6.first, f32[16,16,128]{2,1,0:T(8,128)S(1)} %collective-permute-done.7.second, f32[16,16,128]{2,1,0:T(8,128)S(1)} %collective-permute-done.8.third), custom_call_target="tpu_custom_call" | custom-call | flops 1048576 | bytes 1048576 | tf_op jit(solution)/shard_map/finish/pallas_call | solution.py:369
  (22 shorter events, 0.0 us)
Async XLA Ops:
  0.6 1.0 %copy-start = (f32[16,32,256]{2,1,0:T(8,128)S(1)}, f32[16,32,256]{2,1,0:T(8,128)}, u32[]{:S(2)}) copy-start(f32[16,32,256]{2,1,0:T(8,128)} %cour.5) | copy-start | bytes 1572868
  1.7 1.2 %copy-start.2 = (f32[2,16,32,256]{3,2,1,0:T(8,128)S(1)}, f32[2,16,32,256]{3,2,1,0:T(8,128)}, u32[]{:S(2)}) copy-start(f32[2,16,32,256]{3,2,1,0:T(8,128)} %a_old.3) | copy-start | bytes 3145732
  2.9 1.2 %copy-start.4 = (f32[2,16,32,256]{3,2,1,0:T(8,128)S(1)}, f32[2,16,32,256]{3,2,1,0:T(8,128)}, u32[]{:S(2)}) copy-start(f32[2,16,32,256]{3,2,1,0:T(8,128)} %u_old.3) | copy-start | bytes 3145732
  4.1 4.7 %copy-start.7 = (f32[2,128,1024]{2,1,0:T(8,128)S(1)}, f32[2,128,1024]{2,1,0:T(8,128)}, u32[]{:S(2)}) copy-start(f32[2,128,1024]{2,1,0:T(8,128)} %trace_hbm.3) | copy-start | bytes 3145732
  4.1 4.7 %copy-start.8 = (f32[2,16,32,256]{3,2,1,0:T(8,128)S(1)}, f32[2,16,32,256]{3,2,1,0:T(8,128)}, u32[]{:S(2)}) copy-start(f32[2,16,32,256]{3,2,1,0:T(8,128)} %u_old.2) | copy-start | bytes 3145732
  4.1 4.7 %copy-start.11 = (s32[2,1024]{1,0:T(2,128)S(1)}, s32[2,1024]{1,0:T(2,128)}, u32[]{:S(2)}) copy-start(s32[2,1024]{1,0:T(2,128)} %rec_ref.3) | copy-start | bytes 24580
  4.8 13.0 %collective-permute-start.2 = (f32[2,2,4,32,256]{4,3,2,1,0:T(8,128)S(1)}, f32[2,2,4,32,256]{4,3,2,1,0:T(8,128)S(1)}, u32[]{:S(2)}, u32[]{:S(2)}) collective-permute-start(f32[2,2,4,32,256]{4,3,2,1,0:T(8,128)S(1)} %get-tuple-element.28), channel_id=1, source_target_pairs={{0,4},{4,0},{1,5},{5,1},{2,6},{6,2},{3,7},{7,3},{8,12},{12,8},{9,1... | collective-permute-start | bytes 1572872 | tf_op jit(solution)/shard_map/ppermute | solution.py:414
  5.3 3.5 %copy-start.14 = (s32[2]{0:T(128)S(1)}, s32[2]{0:T(128)}, u32[]{:S(2)}) copy-start(s32[2]{0:T(128)} %src_ref.3) | copy-start | bytes 28
  5.4 3.5 %copy-start.12 = (f32[2,128]{1,0:T(2,128)S(1)}, f32[2,128]{1,0:T(2,128)}, u32[]{:S(2)}) copy-start(f32[2,128]{1,0:T(2,128)} %wave_ref.3) | copy-start | bytes 3076
  5.4 3.5 %copy-start.13 = (s32[2]{0:T(128)S(1)}, s32[2]{0:T(128)}, u32[]{:S(2)}) copy-start(s32[2]{0:T(128)} %step_ref.3) | copy-start | bytes 28
  5.4 12.4 %collective-permute-start = (f32[2,16,8,256]{3,2,1,0:T(8,128)S(1)}, f32[2,16,8,256]{3,2,1,0:T(8,128)S(1)}, u32[]{:S(2)}, u32[]{:S(2)}) collective-permute-start(f32[2,16,8,256]{3,2,1,0:T(8,128)S(1)} %get-tuple-element.26), channel_id=1, source_target_pairs={{0,1},{2,3},{1,0},{3,2},{4,5},{6,7},{5,4},{7,6},{8,9},{10,11},{9,8... | collective-permute-start | bytes 786440 | tf_op jit(solution)/shard_map/ppermute | solution.py:413
  8.0 9.7 %copy-start.1 = (f32[16,32,256]{2,1,0:T(8,128)S(1)}, f32[16,32,256]{2,1,0:T(8,128)}, u32[]{:S(2)}) copy-start(f32[16,32,256]{2,1,0:T(8,128)} %cour.5) | copy-start | bytes 1572868
  8.0 9.7 %copy-start.3 = (f32[2,16,32,256]{3,2,1,0:T(8,128)S(1)}, f32[2,16,32,256]{3,2,1,0:T(8,128)}, u32[]{:S(2)}) copy-start(f32[2,16,32,256]{3,2,1,0:T(8,128)} %a_old.3) | copy-start | bytes 3145732
  8.0 9.7 %collective-permute-start.1 = (f32[2,16,8,256]{3,2,1,0:T(8,128)S(1)}, f32[2,16,8,256]{3,2,1,0:T(8,128)S(1)}, u32[]{:S(2)}, u32[]{:S(2)}) collective-permute-start(f32[2,16,8,256]{3,2,1,0:T(8,128)S(1)} %get-tuple-element.27), channel_id=1, source_target_pairs={{1,2},{2,1},{5,6},{6,5},{9,10},{10,9},{13,14},{14,13},{17,18},{18,... | collective-permute-start | bytes 786440 | tf_op jit(solution)/shard_map/ppermute | solution.py:413
  8.9 1.2 %copy-start.9 = (f32[2,16,32,256]{3,2,1,0:T(8,128)S(1)}, f32[2,16,32,256]{3,2,1,0:T(8,128)}, u32[]{:S(2)}) copy-start(f32[2,16,32,256]{3,2,1,0:T(8,128)} %a_old.2) | copy-start | bytes 3145732
  20.2 15.2 %collective-permute-start.5 = (f32[2,2,4,32,256]{4,3,2,1,0:T(8,128)S(1)}, f32[2,2,4,32,256]{4,3,2,1,0:T(8,128)S(1)}, u32[]{:S(2)}, u32[]{:S(2)}) collective-permute-start(f32[2,2,4,32,256]{4,3,2,1,0:T(8,128)S(1)} %get-tuple-element.35), channel_id=1, source_target_pairs={{0,4},{4,0},{1,5},{5,1},{2,6},{6,2},{3,7},{7,3},{8,12},{12,8},{9,1... | collective-permute-start | bytes 1572872 | tf_op jit(solution)/shard_map/ppermute | solution.py:414
  20.3 15.1 %collective-permute-start.3 = (f32[2,16,8,256]{3,2,1,0:T(8,128)S(1)}, f32[2,16,8,256]{3,2,1,0:T(8,128)S(1)}, u32[]{:S(2)}, u32[]{:S(2)}) collective-permute-start(f32[2,16,8,256]{3,2,1,0:T(8,128)S(1)} %get-tuple-element.33), channel_id=1, source_target_pairs={{0,1},{2,3},{1,0},{3,2},{4,5},{6,7},{5,4},{7,6},{8,9},{10,11},{9,8... | collective-permute-start | bytes 786440 | tf_op jit(solution)/shard_map/ppermute | solution.py:413
  24.6 10.8 %collective-permute-start.4 = (f32[2,16,8,256]{3,2,1,0:T(8,128)S(1)}, f32[2,16,8,256]{3,2,1,0:T(8,128)S(1)}, u32[]{:S(2)}, u32[]{:S(2)}) collective-permute-start(f32[2,16,8,256]{3,2,1,0:T(8,128)S(1)} %get-tuple-element.34), channel_id=1, source_target_pairs={{1,2},{2,1},{5,6},{6,5},{9,10},{10,9},{13,14},{14,13},{17,18},{18,... | collective-permute-start | bytes 786440 | tf_op jit(solution)/shard_map/ppermute | solution.py:413
  25.2 1.2 %copy-start.5 = (f32[2,16,32,256]{3,2,1,0:T(8,128)S(1)}, f32[2,16,32,256]{3,2,1,0:T(8,128)}, u32[]{:S(2)}) copy-start(f32[2,16,32,256]{3,2,1,0:T(8,128)} %get-tuple-element.23.a.refs_3_) | copy-start | bytes 3145732
  26.5 1.2 %copy-start.10 = (f32[2,16,32,256]{3,2,1,0:T(8,128)S(1)}, f32[2,16,32,256]{3,2,1,0:T(8,128)}, u32[]{:S(2)}) copy-start(f32[2,16,32,256]{3,2,1,0:T(8,128)} %get-tuple-element.21.u) | copy-start | bytes 3145732
  27.7 7.7 %copy-start.6 = (f32[2,16,32,256]{3,2,1,0:T(8,128)S(1)}, f32[2,16,32,256]{3,2,1,0:T(8,128)}, u32[]{:S(2)}) copy-start(f32[2,16,32,256]{3,2,1,0:T(8,128)} %get-tuple-element.23.a.refs_3_) | copy-start | bytes 3145732
  39.2 6.0 %collective-permute-start.6 = (f32[16,16,128]{2,1,0:T(8,128)S(1)}, f32[16,16,128]{2,1,0:T(8,128)S(1)}, u32[]{:S(2)}, u32[]{:S(2)}) collective-permute-start(f32[16,16,128]{2,1,0:T(8,128)S(1)} %get-tuple-element.44), channel_id=1, source_target_pairs={{0,8},{8,0},{16,24},{24,16},{1,9},{9,1},{17,25},{25,17},{2,10},{10... | collective-permute-start | bytes 393224 | tf_op jit(solution)/shard_map/ppermute | solution.py:443
  40.7 8.2 %collective-permute-start.7 = (f32[16,16,128]{2,1,0:T(8,128)S(1)}, f32[16,16,128]{2,1,0:T(8,128)S(1)}, u32[]{:S(2)}, u32[]{:S(2)}) collective-permute-start(f32[16,16,128]{2,1,0:T(8,128)S(1)} %get-tuple-element.45), channel_id=1, source_target_pairs={{0,16},{8,24},{16,0},{24,8},{1,17},{9,25},{17,1},{25,9},{2,18},{10... | collective-permute-start | bytes 393224 | tf_op jit(solution)/shard_map/ppermute | solution.py:443
  42.2 6.6 %collective-permute-start.8 = (f32[16,16,128]{2,1,0:T(8,128)S(1)}, f32[16,16,128]{2,1,0:T(8,128)S(1)}, u32[]{:S(2)}, u32[]{:S(2)}) collective-permute-start(f32[16,16,128]{2,1,0:T(8,128)S(1)} %get-tuple-element.46), channel_id=1, source_target_pairs={{0,24},{8,16},{16,8},{24,0},{1,25},{9,17},{17,9},{25,1},{2,26},{10... | collective-permute-start | bytes 393224 | tf_op jit(solution)/shard_map/ppermute | solution.py:443

commit v2 on v1

--- a/solution.py
+++ b/solution.py
@@ -12,9 +12,10 @@
 REC_DEPTH = 6
 COEFS = (-205.0 / 72.0, 8.0 / 5.0, -1.0 / 5.0, 8.0 / 315.0, -1.0 / 560.0)
 F32 = jnp.float32
+BF16 = jnp.bfloat16
 VMEM = pl.BlockSpec(memory_space=pltpu.VMEM)
 SMEM = pl.BlockSpec(memory_space=pltpu.SMEM)
-ANY = pl.BlockSpec(memory_space=pl.ANY)
+HBM = pl.BlockSpec(memory_space=pltpu.HBM)
 
 
 def iota(dim):
@@ -25,19 +26,42 @@
     return lax.axis_index(axis) % 2 == 0
 
 
-def pair_permutes(axis):
-    count = lax.axis_size(axis)
+def pair_permutes(axis, other):
+    count, across = lax.axis_size(axis), lax.axis_size(other)
     perms = []
+
+    def at(i, j):
+        return i * across + j if axis == "gx" else j * count + i
+
     for first in (0, 1):
         pairs = [(i, i + 1) for i in range(first, count - 1, 2)]
-        if pairs:
-            perms.append(pairs + [(b, a) for a, b in pairs])
+        if not pairs:
+            continue
+        left = set(range(count)) - {i for pair in pairs for i in pair}
+        perm = [(at(a, j), at(b, j)) for a, b in pairs for j in range(across)]
+        perm += [(b, a) for a, b in perm]
+        if across % 2 == 0:
+            perm += [(at(i, j), at(i, j ^ 1)) for i in sorted(left) for j in range(across)]
+        perms.append(perm)
     return perms
+
+
+def has_neighbour(axis, step):
+    at = lax.axis_index(axis) + step
+    return (at >= 0) & (at < lax.axis_size(axis))
 
 
 def edge_layer(axis, width, turn, k):
     high = even_on(axis) if turn == 0 else jnp.logical_not(even_on(axis))
     return jnp.where(high, width - 1 - k, k)
+
+
+def in_hbm(x):
+    return pltpu.with_memory_space_constraint(x, pltpu.HBM)
+
+
+def in_vmem(x):
+    return pltpu.with_memory_space_constraint(x, pltpu.VMEM)
 
 
 def halves(depth):
@@ -98,7 +122,7 @@
                 )
         return carry
 
-    lax.fori_loop(0, width_x, line, 0)
+    lax.fori_loop(0, width_x, line, 0, unroll=4)
     for turn in range(turns_x):
         top = edge_layer("gx", width_x, turn, 0) > 3
         for k in range(4):
@@ -109,37 +133,61 @@
                 xs[turn][1, s, k] = mass * a_x[turn, s, layer]
 
 
-def laplace_tile(field, s, x, row):
-    lane = iota(1)
-    center = [field[s, h, x + 4, pl.ds(row, 8), :] for h in range(2)]
-    total = [3.0 * COEFS[0] * c for c in center]
+def depth_band(depth):
+    apart = jnp.abs(
+        lax.broadcasted_iota(jnp.int32, (depth, depth), 0)
+        - lax.broadcasted_iota(jnp.int32, (depth, depth), 1)
+    )
+    band = jnp.zeros((depth, depth), F32)
     for r in range(1, 5):
-        right = [pltpu.roll(c, r, 1) for c in center]
-        left = [pltpu.roll(c, 128 - r, 1) for c in center]
-        low, high = lane < r, lane >= 128 - r
-        deep = [
-            jnp.where(low, 0.0, right[0]) + jnp.where(high, left[1], left[0]),
-            jnp.where(low, right[0], right[1]) + jnp.where(high, 0.0, left[1]),
-        ]
-        for h in range(2):
+        band = jnp.where(apart == r, float(round(5040 * COEFS[r])), band)
+    return band.astype(BF16)
+
+
+def three_parts(v):
+    top = v.astype(BF16)
+    rest = v - top.astype(F32)
+    middle = rest.astype(BF16)
+    return top, middle, (rest - middle.astype(F32)).astype(BF16)
+
+
+def laplace_tile(field, deep, s, x, row):
+    totals, centers = [], []
+    for h in range(2):
+        center = field[s, h, x + 4, pl.ds(row, 8), :]
+        total = 3.0 * COEFS[0] * center + deep[:, h * 128 : h * 128 + 128]
+        for r in range(1, 5):
             part = field[s, h, x + 4 + r, pl.ds(row, 8), :] + field[s, h, x + 4 - r, pl.ds(row, 8), :]
             part = part + field[s, h, x + 4, pl.ds(row + r, 8), :] + field[s, h, x + 4, pl.ds(row - r, 8), :]
-            total[h] = total[h] + COEFS[r] * (part + deep[h])
-    return center, total
-
-
-def march(offset, rows_y, step_ref, src_ref, wave_ref, rec_ref, trace_hbm, u, u_old, a, a_old, cour, *refs):
+            total = total + COEFS[r] * part
+        centers.append(center)
+        totals.append(total)
+    return centers, totals
+
+
+def march(offset, rows_y, step_ref, src_ref, wave_ref, rec_hbm, trace_hbm, u, u_old, a, a_old, cour, *refs):
     image_in, refs = (refs[0], refs[1:]) if offset else (None, refs)
-    u_out, a_out, image, field_u, field_m, trace, sems = refs
+    u_out, a_out, image, *refs = refs
+    priors, refs = (refs[:2], refs[2:]) if offset else ((), refs)
+    field_u, field_m, split, band, deep, trace, rec_ref, *olds, sems = refs
     shots, width_x, width_y, depth = u.shape
     tiles = width_y // 8
     copies = []
+
+    def move(src, dst):
+        copy = pltpu.make_async_copy(src, dst, sems.at[len(copies)])
+        copy.start()
+        copies.append(copy)
+        return copy
+
+    loads = [move(src, dst) for src, dst in zip((u_old, a_old), olds)]
+    saves = [move(src, dst) for src, dst in zip((u, a), priors)]
+    late = [move(rec_hbm, rec_ref)]
+    u_old, a_old = olds or (u_old, a_old)
     for s in range(shots):
         moment = step_ref[s] - offset
         block = pl.multiple_of((moment // 8) * 8, 8)
-        copy = pltpu.make_async_copy(trace_hbm.at[s, pl.ds(block, 8), :], trace.at[s], sems.at[s])
-        copy.start()
-        copies.append(copy)
+        late.append(move(trace_hbm.at[s, pl.ds(block, 8), :], trace.at[s]))
     zero = jnp.zeros((8, 128), F32)
     for field in (field_u, field_m):
         for s in range(shots):
@@ -148,30 +196,42 @@
                     for t in range(1, tiles + 1):
                         field[s, h, x, 8 * t : 8 * t + 8, :] = zero
 
-    def fill(x, carry):
-        for h, z in enumerate(halves(depth)):
-            for t in range(tiles):
-                row = slice(8 * t, 8 * t + 8)
-                mass = cour[x, row, z] * cour[x, row, z]
+    for part in range(3):
+        band[part * depth : part * depth + depth, :] = depth_band(depth)
+
+    def fill(pair, carry):
+        for k in range(2):
+            x = 2 * pair + k
+            mass = cour[x] * cour[x]
+            for f, field in enumerate((field_u, field_m)):
                 for s in range(shots):
-                    field_u[s, h, x + 4, 8 * t + 8 : 8 * t + 16, :] = u[s, x, row, z]
-                    field_m[s, h, x + 4, 8 * t + 8 : 8 * t + 16, :] = mass * a[s, x, row, z]
-            for field in (field_u, field_m):
-                for s in range(shots):
-                    field[s, h, x + 4, 0:8, :] = zero
-                    field[s, h, x + 4, width_y + 8 : width_y + 16, :] = zero
+                    block = mass * a[s, x] if f else u[s, x]
+                    rows = ((k * 2 + f) * shots + s) * width_y
+                    for part, value in enumerate(three_parts(block)):
+                        split[rows : rows + width_y, part * depth : part * depth + depth] = value
+                    for h, z in enumerate(halves(depth)):
+                        field[s, h, x + 4, 0:8, :] = zero
+                        field[s, h, x + 4, 8 : width_y + 8, :] = block[:, z]
+                        field[s, h, x + 4, width_y + 8 : width_y + 16, :] = zero
+        deep[pair] = jnp.dot(split[...], band[...], preferred_element_type=F32) * (1.0 / 5040.0)
         return carry
 
-    lax.fori_loop(0, width_x, fill, 0)
+    lax.fori_loop(0, width_x // 2, fill, 0)
+    for load in loads:
+        load.wait()
 
     def line(x, carry):
+        pair, side = x // 2, x % 2
         for t in range(tiles):
             row = slice(8 * t, 8 * t + 8)
             mass = [cour[x, row, z] * cour[x, row, z] for z in halves(depth)]
             terms = [image_in[h, x, row, :] if offset else None for h in range(2)]
             for s in range(shots):
-                center, lap_u = laplace_tile(field_u, s, x, 8 * t + 8)
-                _, lap_a = laplace_tile(field_m, s, x, 8 * t + 8)
+                laps = []
+                for f, field in enumerate((field_u, field_m)):
+                    at = pl.multiple_of(((side * 2 + f) * shots + s) * width_y + 8 * t, 8)
+                    laps.append(laplace_tile(field, deep[pair, pl.ds(at, 8), :], s, x, 8 * t + 8))
+                (center, lap_u), (_, lap_a) = laps
                 for h, z in enumerate(halves(depth)):
                     a_now = a[s, x, row, z]
                     term = a_now * lap_u[h]
@@ -184,6 +244,8 @@
 
     lax.fori_loop(0, width_x, line, 0)
 
+    for copy in late:
+        copy.wait()
     bits = rows_y.bit_length() - 1
     anchor_x = lax.axis_index("gx") * width_x
     anchor_y = lax.axis_index("gy") * width_y
@@ -202,7 +264,6 @@
             added = jnp.where(hit, speed * speed * wave_ref[s, moment], 0.0)
             u_out[s, place_x, row, 0:128] = u_out[s, place_x, row, 0:128] + added
 
-        copies[s].wait()
         pick = lax.broadcasted_iota(jnp.int32, trace.shape[1:], 0) == moment % 8
         values = jnp.sum(jnp.where(pick, trace[s], 0.0), axis=0, keepdims=True)
         cells = rec_ref[s : s + 1, :]
@@ -211,17 +272,20 @@
         cell_y = (cells & (rows_y - 1)) - anchor_y
         hot_x = lax.broadcasted_iota(jnp.int32, (width_x, count), 0) == cell_x
         hot_y = lax.broadcasted_iota(jnp.int32, (width_y, count), 0) == cell_y
-        plane = lax.dot_general(
-            jnp.where(hot_y, values, 0.0),
-            jnp.where(hot_x, 1.0, 0.0),
+        spread = [jnp.where(hot_y, part.astype(F32), 0.0).astype(BF16) for part in three_parts(values)]
+        planes = lax.dot_general(
+            jnp.concatenate(spread, axis=0),
+            jnp.where(hot_x, 1.0, 0.0).astype(BF16),
             (((1,), (1,)), ((), ())),
-            precision=lax.Precision.HIGHEST,
             preferred_element_type=F32,
         )
+        plane = planes[0:width_y] + planes[width_y : 2 * width_y] + planes[2 * width_y :]
         depth_mask = lax.broadcasted_iota(jnp.int32, (width_y, 128), 1) == REC_DEPTH
         for x in range(width_x):
             added = jnp.where(depth_mask, plane[:, x : x + 1], 0.0)
             a_out[s, x, :, 0:128] = a_out[s, x, :, 0:128] + added
+    for save in saves:
+        save.wait()
 
 
 def packed(load, target, x):
@@ -236,20 +300,12 @@
 def edge(turns_x, turns_y, last, *refs):
     hy, refs = refs[:turns_y], refs[turns_y:]
     hx, refs = refs[:turns_x], refs[turns_x:]
-    a, cour, u_in, a_in, image_in, u_out, a_out, image, *sends = refs
+    a, cour, _, _, _, u_out, a_out, image, *sends = refs
     shots, width_x, width_y, depth = a.shape
     sub = iota(0)
     even = even_on("gy")
 
-    def keep(x, carry):
-        for s in range(shots):
-            u_out[s, x] = u_in[s, x]
-            a_out[s, x] = a_in[s, x]
-        for h in range(2):
-            image[h, x] = image_in[h, x]
-        return carry
-
-    lax.fori_loop(0, width_x, keep, 0)
+    has_below, has_above = has_neighbour("gy", -1), has_neighbour("gy", 1)
 
     def coef(values):
         out = jnp.zeros((8, 128), F32)
@@ -269,8 +325,8 @@
             for s in range(shots):
                 first = hy[0][s, x, :, z]
                 second = hy[1][s, x, :, z] if turns_y > 1 else jnp.zeros_like(first)
-                below = jnp.where(even, second, first)
-                above = jnp.where(even, first, second)
+                below = jnp.where(has_below, jnp.where(even, second, first), 0.0)
+                above = jnp.where(has_above, jnp.where(even, first, second), 0.0)
                 for side in range(2):
                     row = slice(0, 8) if side == 0 else slice(width_y - 8, width_y)
                     lap_u = lap_a = None
@@ -291,8 +347,10 @@
             image[h, x, width_y - 8 : width_y, :] = terms[1]
         return carry
 
-    lax.fori_loop(0, width_x, rows, 0)
+    lax.fori_loop(0, width_x, rows, 0, unroll=2)
     for turn in range(turns_x):
+        toward = jnp.where(even_on("gx"), 1, -1) * (1 if turn == 0 else -1)
+        whole = turn == 0 and lax.axis_size("gx") % 2 == 0
         for j in range(4):
             x = edge_layer("gx", width_x, turn, j)
             for h, z in enumerate(halves(depth)):
@@ -304,6 +362,9 @@
                         part_a = COEFS[j + k + 1] * hx[turn][1, s, k, :, z]
                         lap_u = part_u if lap_u is None else lap_u + part_u
                         lap_a = part_a if lap_a is None else lap_a + part_a
+                    if not whole:
+                        lap_u = jnp.where(has_neighbour("gx", toward), lap_u, 0.0)
+                        lap_a = jnp.where(has_neighbour("gx", toward), lap_a, 0.0)
                     mass = cour[x, :, z] * cour[x, :, z]
                     u_out[s, x, :, z] = u_out[s, x, :, z] + mass * lap_u
                     a_out[s, x, :, z] = a_out[s, x, :, z] + lap_a
@@ -317,7 +378,7 @@
                 ref[x] = packed(lambda h, x: image[h, x], me ^ k, x)
             return carry
 
-        lax.fori_loop(0, width_x, parts, 0)
+        lax.fori_loop(0, width_x, parts, 0, unroll=2)
         return
     ys, xs = sends[:turns_y], sends[turns_y:]
 
@@ -341,7 +402,7 @@
                 )
         return carry
 
-    lax.fori_loop(0, width_x, outgoing, 0)
+    lax.fori_loop(0, width_x, outgoing, 0, unroll=4)
     for turn in range(turns_x):
         for k in range(4):
             x = edge_layer("gx", width_x, turn, k)
@@ -351,6 +412,17 @@
                 xs[turn][1, s, k] = mass * a_out[s, x]
 
 
+def flush(u, a, u_out, a_out, sems):
+    copies = [
+        pltpu.make_async_copy(u, u_out, sems.at[0]),
+        pltpu.make_async_copy(a, a_out, sems.at[1]),
+    ]
+    for copy in copies:
+        copy.start()
+    for copy in copies:
+        copy.wait()
+
+
 def finish(scale, cour, own, first, second, third, out):
     me = lax.axis_index("shot")
 
@@ -362,17 +434,18 @@
         out[x, 16:32, :] = value[:, 64:128]
         return carry
 
-    lax.fori_loop(0, out.shape[0], line, 0)
-
-
-def call(body, name, outs, scratch, in_specs, args, cost, limit=40 << 20):
+    lax.fori_loop(0, out.shape[0], line, 0, unroll=4)
+
+
+def call(body, name, outs, scratch, in_specs, args, cost, aliases=None, out_specs=None, limit=24 << 20):
     return pl.pallas_call(
         body,
         name=name,
         out_shape=outs,
         in_specs=in_specs,
-        out_specs=[VMEM] * len(outs),
+        out_specs=out_specs or [VMEM] * len(outs),
         scratch_shapes=scratch,
+        input_output_aliases=aliases or {},
         compiler_params=pltpu.CompilerParams(vmem_limit_bytes=limit),
         cost_estimate=pl.CostEstimate(flops=cost, bytes_accessed=cost, transcendentals=0),
     )(*args)
@@ -385,7 +458,7 @@
     groups = lax.axis_size("shot")
     rows_y = width_y * lax.axis_size("gy")
     assert rows_y & (rows_y - 1) == 0 and depth == 256 and groups == 4 and width_y == 32
-    perms_x, perms_y = pair_permutes("gx"), pair_permutes("gy")
+    perms_x, perms_y = pair_permutes("gx", "gy"), pair_permutes("gy", "gx")
     turns_x, turns_y = len(perms_x), len(perms_y)
 
     def shape(*dims):
@@ -402,30 +475,48 @@
         "first_sends",
         send_shapes,
         scratch,
-        [ANY] * 3,
-        (fwd_now, adj_now, courant),
+        [HBM] * 3,
+        (in_hbm(fwd_now), in_hbm(adj_now), in_hbm(courant)),
         1 << 20,
     )
     u_now, u_next, a_now, a_next = fwd_now, fwd_next, adj_now, adj_next
     image = None
     for offset in range(STEPS):
         last = offset == STEPS - 1
-        halo_y = [lax.ppermute(s, "gy", p) for s, p in zip(sends[:turns_y], perms_y)]
-        halo_x = [lax.ppermute(s, "gx", p) for s, p in zip(sends[turns_y:], perms_x)]
+        halo_y = [lax.ppermute(s, ("gx", "gy"), p) for s, p in zip(sends[:turns_y], perms_y)]
+        halo_x = [lax.ppermute(s, ("gx", "gy"), p) for s, p in zip(sends[turns_y:], perms_x)]
         padded = pltpu.VMEM((shots, 2, width_x + 8, width_y + 16, 128), F32)
-        args = (step_index, src_cells, wavelet, rec_cells, traces, u_now, u_next, a_now, a_next, courant)
+        old = (u_next, a_next) if offset else (in_hbm(u_next), in_hbm(a_next))
+        args = (step_index, src_cells, wavelet, in_hbm(rec_cells), in_hbm(traces))
+        args += (u_now, old[0], a_now, old[1], courant)
         args += (image,) if offset else ()
         state = [shape(*fwd_now.shape)] * 2 + [shape(2, width_x, width_y, 128)]
-        u_prev, a_prev, image = call(
+        priors = [shape(*fwd_now.shape)] * 2 if offset else []
+        u_prev, a_prev, image, *priors = call(
             functools.partial(march, offset, rows_y),
             f"march_{offset}",
-            state,
-            [padded, padded, pltpu.VMEM((shots, 8, traces.shape[-1]), F32), pltpu.SemaphoreType.DMA((shots,))],
-            [SMEM] * 3 + [VMEM, ANY] + [VMEM] * (len(args) - 5),
+            state + priors,
+            [
+                padded,
+                padded,
+                pltpu.VMEM((4 * shots * width_y, 3 * depth), BF16),
+                pltpu.VMEM((3 * depth, depth), BF16),
+                pltpu.VMEM((width_x // 2, 4 * shots * width_y, depth), F32),
+                pltpu.VMEM((shots, 8, traces.shape[-1]), F32),
+                pltpu.VMEM(rec_cells.shape, jnp.int32),
+                *([] if offset else [pltpu.VMEM(fwd_now.shape, F32)] * 2),
+                pltpu.SemaphoreType.DMA((shots + 3,)),
+            ],
+            [SMEM] * 3
+            + [HBM] * 2
+            + ([VMEM] * 4 if offset else [VMEM, HBM] * 2)
+            + [VMEM] * (len(args) - 9),
             args,
             16 << 20,
+            out_specs=[VMEM] * 3 + [HBM] * len(priors),
         )
-        args = (*halo_y, *halo_x, a_now, courant, u_prev, a_prev, image)
+        args = (*halo_y, *halo_x, a_now, courant, in_vmem(u_prev), in_vmem(a_prev), in_vmem(image))
+        base = len(args) - 3
         outs = state + ([shape(width_x, 16, 128)] * groups if last else send_shapes)
         u_prev, a_prev, image, *sends = call(
             functools.partial(edge, turns_x, turns_y, last),
@@ -435,9 +526,20 @@
             [VMEM] * len(args),
             args,
             2 << 20,
+            {base: 0, base + 1: 1, base + 2: 2},
         )
         u_next, u_now = u_now, u_prev
         a_next, a_now = a_now, a_prev
+    starts = call(
+        flush,
+        "flush",
+        [shape(*fwd_now.shape)] * 2,
+        [pltpu.SemaphoreType.DMA((2,))],
+        [VMEM] * 2,
+        (in_vmem(u_now), in_vmem(a_now)),
+        4 << 20,
+        out_specs=[HBM] * 2,
+    )
     parts = [sends[0]]
     for k in range(1, groups):
         parts.append(lax.ppermute(sends[k], "shot", [(i, i ^ k) for i in range(groups)]))
@@ -450,7 +552,7 @@
         (courant, *parts),
         1 << 20,
     )
-    return (u_next, u_now, a_next, a_now, gradient)
+    return (priors[0], starts[0], priors[1], starts[1], gradient)
 
 
 def solution(mesh):

time: 52.4 us -> 37.7 us (0.72)
  local copies, waits for them, and re-layouts: 7.18 us -> 0.02 us
  Pallas kernels: 25.2 us -> 21.6 us
  starting transfers between devices: 12.6 us -> 10.2 us
  waiting for transfers between devices: 6.19 us -> 4.98 us
    unnamed x30 -> x12, local copies, waits for them, and re-layouts: 7.18 us -> 0.02 us
    pallas_call x6 -> x7, Pallas kernels: 25.2 us -> 21.6 us  [call(): pl.pallas_call(body, name=name, out_shape=outs, in_specs=in_specs, out_sp...]
    ppermute x6, starting transfers between devices: 9.08 us -> 6.68 us  [shards(): lax.ppermute(s, ('gx', 'gy'), p)]
    ppermute x3, waiting for transfers between devices: 6.17 us -> 4.97 us  [shards(): lax.ppermute(sends[k], 'shot', [(i, i ^ k) for i in range(groups)])]
  transfers between devices with their start and end apart: 9 -> 9, of which waited for: 2 -> 2; matrix products, arithmetic and copies ran while one was open for 0% -> 0% of each run, Pallas kernels for 29% -> 42%
where the time goes in v2:
time: 37.7 us; the launch traced here: 37.6 us
  Pallas kernels  21.6 us (57%)
  starting transfers between devices  10.2 us (27%)
  waiting for transfers between devices  4.98 us (13%)
  between operations  0.77 us (2%)
    pallas_call x7, Pallas kernels, call(): pl.pallas_call(body, name=name, out_shape=outs, in_specs=in_specs, out_sp...  21.6 us
    ppermute x6, starting transfers between devices, shards(): lax.ppermute(s, ('gx', 'gy'), p)  6.68 us
    ppermute x3, waiting for transfers between devices, shards(): lax.ppermute(sends[k], 'shot', [(i, i ^ k) for i in range(groups)])  4.97 us
    ppermute x3, starting transfers between devices, shards(): lax.ppermute(sends[k], 'shot', [(i, i ^ k) for i in range(groups)])  3.55 us
  transfers between devices with their start and end apart: 9, of which 2 were waited for; matrix products, arithmetic and copies ran while one was open for 0% of the time, Pallas kernels for 42%

profile of v2, /device:TPU:0, one launch (start us, length us, event | category | flops | bytes accessed | tf_op | source)
XLA Modules:
  0.0 37.6 jit_solution(15205251963024938097)
XLA Ops:
  0.6 0.0 copy-start
  0.6 0.0 copy-start.1
  0.7 0.0 copy-start.2
  0.7 1.8 %first_sends.1 = (f32[2,16,8,256]{3,2,1,0:T(8,128)S(1)}, f32[2,16,8,256]{3,2,1,0:T(8,128)S(1)}, f32[2,2,4,32,256]{4,3,2,1,0:T(8,128)S(1)}) custom-call(f32[2,16,32,256]{3,2,1,0:T(8,128)} %u_old.3, f32[2,16,32,256]{3,2,1,0:T(8,128)} %a_old.3, f32[16,32,256]{2,1,0:T(8,128)} %cour.5), custom_call_target="tpu_custom_call" | custom-call | flops 1048576 | bytes 1048576 | tf_op jit(solution)/shard_map/first_sends/pallas_call | solution.py:441
  2.5 0.6 %collective-permute-start.2 = (f32[2,2,4,32,256]{4,3,2,1,0:T(8,128)S(1)}, f32[2,2,4,32,256]{4,3,2,1,0:T(8,128)S(1)}, u32[]{:S(2)}, u32[]{:S(2)}) collective-permute-start(f32[2,2,4,32,256]{4,3,2,1,0:T(8,128)S(1)} %get-tuple-element.32), channel_id=1, source_target_pairs={{0,4},{1,5},{2,6},{3,7},{4,0},{5,1},{6,2},{7,3},{8,12},{9,13},{10,... | collective-permute-start | bytes 1572872 | tf_op jit(solution)/shard_map/ppermute | solution.py:487
  3.1 2.7 %collective-permute-start = (f32[2,16,8,256]{3,2,1,0:T(8,128)S(1)}, f32[2,16,8,256]{3,2,1,0:T(8,128)S(1)}, u32[]{:S(2)}, u32[]{:S(2)}) collective-permute-start(f32[2,16,8,256]{3,2,1,0:T(8,128)S(1)} %get-tuple-element.30), channel_id=1, source_target_pairs={{0,1},{4,5},{2,3},{6,7},{1,0},{5,4},{3,2},{7,6},{8,9},{12,13},{10,... | collective-permute-start | bytes 786440 | tf_op jit(solution)/shard_map/ppermute | solution.py:486
  5.7 0.1 collective-permute-start.1
  5.9 0.0 copy-done
  5.9 0.0 copy-done.1
  5.9 0.0 copy-done.2
  5.9 0.0 copy-done.5
  5.9 7.3 %march_0.1 = (f32[2,16,32,256]{3,2,1,0:T(8,128)S(1)}, f32[2,16,32,256]{3,2,1,0:T(8,128)S(1)}, f32[2,16,32,128]{3,2,1,0:T(8,128)S(1)}) custom-call(s32[2]{0:T(128)S(1)} %copy-done.4, s32[2]{0:T(128)S(1)} %copy-done.5, f32[2,128]{1,0:T(2,128)S(1)} %copy-done.3, s32[2,1024]{1,0:T(2,128)} %rec_hbm.3, f32[2,128,1024]{2,1,0:T(8,128)} %trace_hbm.3, ...), custom_call_target="tpu_custom_call" | custom-call | flops 16777216 | bytes 16777216 | tf_op jit(solution)/shard_map/march_0/pallas_call | solution.py:441
  13.2 0.0 collective-permute-done.refs_0_
  13.2 0.0 collective-permute-done.1.refs_1_
  13.2 0.0 collective-permute-done.2.refs_2_
  13.2 0.9 %edge_0.1 = (f32[2,16,32,256]{3,2,1,0:T(8,128)S(1)}, f32[2,16,32,256]{3,2,1,0:T(8,128)S(1)}, f32[2,16,32,128]{3,2,1,0:T(8,128)S(1)}, f32[2,16,8,256]{3,2,1,0:T(8...) custom-call(f32[2,16,8,256]{3,2,1,0:T(8,128)S(1)} %collective-permut, ...), custom_call_target="tpu_custom_call", output_to_operand_aliasing={{0}: (5, {}), {1}: (6, {}), {2}: (7, {})} | custom-call | flops 2097152 | bytes 2097152 | tf_op jit(solution)/shard_map/edge_0/pallas_call | solution.py:441
  14.1 0.5 %collective-permute-start.5 = (f32[2,2,4,32,256]{4,3,2,1,0:T(8,128)S(1)}, f32[2,2,4,32,256]{4,3,2,1,0:T(8,128)S(1)}, u32[]{:S(2)}, u32[]{:S(2)}) collective-permute-start(f32[2,2,4,32,256]{4,3,2,1,0:T(8,128)S(1)} %get-tuple-element.42), channel_id=1, source_target_pairs={{0,4},{1,5},{2,6},{3,7},{4,0},{5,1},{6,2},{7,3},{8,12},{9,13},{10,... | collective-permute-start | bytes 1572872 | tf_op jit(solution)/shard_map/ppermute | solution.py:487
  14.5 2.7 %collective-permute-start.3 = (f32[2,16,8,256]{3,2,1,0:T(8,128)S(1)}, f32[2,16,8,256]{3,2,1,0:T(8,128)S(1)}, u32[]{:S(2)}, u32[]{:S(2)}) collective-permute-start(f32[2,16,8,256]{3,2,1,0:T(8,128)S(1)} %get-tuple-element.40), channel_id=1, source_target_pairs={{0,1},{4,5},{2,3},{6,7},{1,0},{5,4},{3,2},{7,6},{8,9},{12,13},{10,... | collective-permute-start | bytes 786440 | tf_op jit(solution)/shard_map/ppermute | solution.py:486
  17.3 0.2 collective-permute-start.4
  17.4 7.4 %march_1.1 = (f32[2,16,32,256]{3,2,1,0:T(8,128)S(1)}, f32[2,16,32,256]{3,2,1,0:T(8,128)S(1)}, f32[2,16,32,128]{3,2,1,0:T(8,128)S(1)}, f32[2,16,32,256]{3,2,1,0:T(8,128)}, f32[2,16,32,256]{3,2,1,0:T(8,128)}) custom-call(s32[2]{0:T(128)S(1)} %copy-done.4, s32[2]{0:T(128)S(1)} %copy-done.5, f32[2,128]{1,0:T(2,128)S(1)} %copy-done.3, s32[2,1024]{1,0:T(2,128)} %rec_hbm.3, ...), custom_call_target="tpu_custom_call" | custom-call | flops 16777216 | bytes 16777216 | tf_op jit(solution)/shard_map/march_1/pallas_call | solution.py:441
  24.8 0.0 collective-permute-done.3.refs_0_
  24.8 0.0 collective-permute-done.4.refs_1_
  24.8 0.0 collective-permute-done.5.refs_2_
  24.8 1.6 %edge_1.1 = (f32[2,16,32,256]{3,2,1,0:T(8,128)S(1)}, f32[2,16,32,256]{3,2,1,0:T(8,128)S(1)}, f32[2,16,32,128]{3,2,1,0:T(8,128)S(1)}, f32[16,16,128]{2,1,0:T(8,12...) custom-call(f32[2,16,8,256]{3,2,1,0:T(8,128)S(1)} %collective-permut, ...), custom_call_target="tpu_custom_call", output_to_operand_aliasing={{0}: (5, {}), {1}: (6, {}), {2}: (7, {})} | custom-call | flops 2097152 | bytes 2097152 | tf_op jit(solution)/shard_map/edge_1/pallas_call | solution.py:441
  26.4 1.6 %collective-permute-start.6 = (f32[16,16,128]{2,1,0:T(8,128)S(1)}, f32[16,16,128]{2,1,0:T(8,128)S(1)}, u32[]{:S(2)}, u32[]{:S(2)}) collective-permute-start(f32[16,16,128]{2,1,0:T(8,128)S(1)} %get-tuple-element.52), channel_id=1, source_target_pairs={{0,8},{8,0},{16,24},{24,16},{1,9},{9,1},{17,25},{25,17},{2,10},{10... | collective-permute-start | bytes 393224 | tf_op jit(solution)/shard_map/ppermute | solution.py:545
  27.9 1.5 %collective-permute-start.7 = (f32[16,16,128]{2,1,0:T(8,128)S(1)}, f32[16,16,128]{2,1,0:T(8,128)S(1)}, u32[]{:S(2)}, u32[]{:S(2)}) collective-permute-start(f32[16,16,128]{2,1,0:T(8,128)S(1)} %get-tuple-element.53), channel_id=1, source_target_pairs={{0,16},{8,24},{16,0},{24,8},{1,17},{9,25},{17,1},{25,9},{2,18},{10... | collective-permute-start | bytes 393224 | tf_op jit(solution)/shard_map/ppermute | solution.py:545
  29.5 0.5 %collective-permute-start.8 = (f32[16,16,128]{2,1,0:T(8,128)S(1)}, f32[16,16,128]{2,1,0:T(8,128)S(1)}, u32[]{:S(2)}, u32[]{:S(2)}) collective-permute-start(f32[16,16,128]{2,1,0:T(8,128)S(1)} %get-tuple-element.54), channel_id=1, source_target_pairs={{0,24},{8,16},{16,8},{24,0},{1,25},{9,17},{17,9},{25,1},{2,26},{10... | collective-permute-start | bytes 393224 | tf_op jit(solution)/shard_map/ppermute | solution.py:545
  29.9 1.3 %flush.1 = (f32[2,16,32,256]{3,2,1,0:T(8,128)}, f32[2,16,32,256]{3,2,1,0:T(8,128)}) custom-call(f32[2,16,32,256]{3,2,1,0:T(8,128)S(1)} %get-tuple-element.46.u, f32[2,16,32,256]{3,2,1,0:T(8,128)S(1)} %get-tuple-element.47.a), custom_call_target="tpu_custom_call" | custom-call | flops 4194304 | bytes 4194304 | tf_op jit(solution)/shard_map/flush/pallas_call | solution.py:441
  31.3 1.3 %collective-permute-done.6.first = f32[16,16,128]{2,1,0:T(8,128)S(1)} collective-permute-done((f32[16,16,128]{2,1,0:T(8,128)S(1)}, f32[16,16,128]{2,1,0:T(8,128)S(1)}, u32[]{:S(2)}, u32[]{:S(2)}) %collective-permute-start.6) | collective-permute-done | bytes 131104 | tf_op jit(solution)/shard_map/ppermute | solution.py:545
  32.6 3.6 %collective-permute-done.7.second = f32[16,16,128]{2,1,0:T(8,128)S(1)} collective-permute-done((f32[16,16,128]{2,1,0:T(8,128)S(1)}, f32[16,16,128]{2,1,0:T(8,128)S(1)}, u32[]{:S(2)}, u32[]{:S(2)}) %collective-permute-start.7) | collective-permute-done | bytes 131104 | tf_op jit(solution)/shard_map/ppermute | solution.py:545
  36.2 0.0 collective-permute-done.8.third
  36.2 1.4 %finish.1 = f32[16,32,64]{2,1,0:T(8,128)} custom-call(f32[16,32,256]{2,1,0:T(8,128)S(1)} %copy-done, f32[16,16,128]{2,1,0:T(8,128)S(1)} %get-tuple-element.51.own, f32[16,16,128]{2,1,0:T(8,128)S(1)} %collective-permute-done.6.first, f32[16,16,128]{2,1,0:T(8,128)S(1)} %collective-permute-done.7.second, f32[16,16,128]{2,1,0:T(8,128)S(1)} %collective-permute-done.8.third), custom_call_target="tpu_custom_call" | custom-call | flops 1048576 | bytes 1048576 | tf_op jit(solution)/shard_map/finish/pallas_call | solution.py:441
  (5 shorter events, 0.0 us)
Async XLA Ops:
  0.6 5.2 %copy-start = (f32[16,32,256]{2,1,0:T(8,128)S(1)}, f32[16,32,256]{2,1,0:T(8,128)}, u32[]{:S(2)}) copy-start(f32[16,32,256]{2,1,0:T(8,128)} %cour.5) | copy-start | bytes 1572868
  0.6 5.2 %copy-start.1 = (f32[2,16,32,256]{3,2,1,0:T(8,128)S(1)}, f32[2,16,32,256]{3,2,1,0:T(8,128)}, u32[]{:S(2)}) copy-start(f32[2,16,32,256]{3,2,1,0:T(8,128)} %a_old.3) | copy-start | bytes 3145732
  0.7 5.2 %copy-start.2 = (f32[2,16,32,256]{3,2,1,0:T(8,128)S(1)}, f32[2,16,32,256]{3,2,1,0:T(8,128)}, u32[]{:S(2)}) copy-start(f32[2,16,32,256]{3,2,1,0:T(8,128)} %u_old.3) | copy-start | bytes 3145732
  2.5 10.7 %collective-permute-start.2 = (f32[2,2,4,32,256]{4,3,2,1,0:T(8,128)S(1)}, f32[2,2,4,32,256]{4,3,2,1,0:T(8,128)S(1)}, u32[]{:S(2)}, u32[]{:S(2)}) collective-permute-start(f32[2,2,4,32,256]{4,3,2,1,0:T(8,128)S(1)} %get-tuple-element.32), channel_id=1, source_target_pairs={{0,4},{1,5},{2,6},{3,7},{4,0},{5,1},{6,2},{7,3},{8,12},{9,13},{10,... | collective-permute-start | bytes 1572872 | tf_op jit(solution)/shard_map/ppermute | solution.py:487
  3.1 2.8 %copy-start.5 = (s32[2]{0:T(128)S(1)}, s32[2]{0:T(128)}, u32[]{:S(2)}) copy-start(s32[2]{0:T(128)} %src_ref.3) | copy-start | bytes 28
  3.1 2.8 %copy-start.3 = (f32[2,128]{1,0:T(2,128)S(1)}, f32[2,128]{1,0:T(2,128)}, u32[]{:S(2)}) copy-start(f32[2,128]{1,0:T(2,128)} %wave_ref.3) | copy-start | bytes 3076
  3.1 2.8 %copy-start.4 = (s32[2]{0:T(128)S(1)}, s32[2]{0:T(128)}, u32[]{:S(2)}) copy-start(s32[2]{0:T(128)} %step_ref.3) | copy-start | bytes 28
  3.1 10.1 %collective-permute-start = (f32[2,16,8,256]{3,2,1,0:T(8,128)S(1)}, f32[2,16,8,256]{3,2,1,0:T(8,128)S(1)}, u32[]{:S(2)}, u32[]{:S(2)}) collective-permute-start(f32[2,16,8,256]{3,2,1,0:T(8,128)S(1)} %get-tuple-element.30), channel_id=1, source_target_pairs={{0,1},{4,5},{2,3},{6,7},{1,0},{5,4},{3,2},{7,6},{8,9},{12,13},{10,... | collective-permute-start | bytes 786440 | tf_op jit(solution)/shard_map/ppermute | solution.py:486
  5.7 7.5 %collective-permute-start.1 = (f32[2,16,8,256]{3,2,1,0:T(8,128)S(1)}, f32[2,16,8,256]{3,2,1,0:T(8,128)S(1)}, u32[]{:S(2)}, u32[]{:S(2)}) collective-permute-start(f32[2,16,8,256]{3,2,1,0:T(8,128)S(1)} %get-tuple-element.31), channel_id=1, source_target_pairs={{1,2},{5,6},{2,1},{6,5},{0,4},{4,0},{3,7},{7,3},{9,10},{13,14},{10... | collective-permute-start | bytes 786440 | tf_op jit(solution)/shard_map/ppermute | solution.py:486
  14.1 10.7 %collective-permute-start.5 = (f32[2,2,4,32,256]{4,3,2,1,0:T(8,128)S(1)}, f32[2,2,4,32,256]{4,3,2,1,0:T(8,128)S(1)}, u32[]{:S(2)}, u32[]{:S(2)}) collective-permute-start(f32[2,2,4,32,256]{4,3,2,1,0:T(8,128)S(1)} %get-tuple-element.42), channel_id=1, source_target_pairs={{0,4},{1,5},{2,6},{3,7},{4,0},{5,1},{6,2},{7,3},{8,12},{9,13},{10,... | collective-permute-start | bytes 1572872 | tf_op jit(solution)/shard_map/ppermute | solution.py:487
  14.5 10.2 %collective-permute-start.3 = (f32[2,16,8,256]{3,2,1,0:T(8,128)S(1)}, f32[2,16,8,256]{3,2,1,0:T(8,128)S(1)}, u32[]{:S(2)}, u32[]{:S(2)}) collective-permute-start(f32[2,16,8,256]{3,2,1,0:T(8,128)S(1)} %get-tuple-element.40), channel_id=1, source_target_pairs={{0,1},{4,5},{2,3},{6,7},{1,0},{5,4},{3,2},{7,6},{8,9},{12,13},{10,... | collective-permute-start | bytes 786440 | tf_op jit(solution)/shard_map/ppermute | solution.py:486
  17.3 7.5 %collective-permute-start.4 = (f32[2,16,8,256]{3,2,1,0:T(8,128)S(1)}, f32[2,16,8,256]{3,2,1,0:T(8,128)S(1)}, u32[]{:S(2)}, u32[]{:S(2)}) collective-permute-start(f32[2,16,8,256]{3,2,1,0:T(8,128)S(1)} %get-tuple-element.41), channel_id=1, source_target_pairs={{1,2},{5,6},{2,1},{6,5},{0,4},{4,0},{3,7},{7,3},{9,10},{13,14},{10... | collective-permute-start | bytes 786440 | tf_op jit(solution)/shard_map/ppermute | solution.py:486
  26.4 6.2 %collective-permute-start.6 = (f32[16,16,128]{2,1,0:T(8,128)S(1)}, f32[16,16,128]{2,1,0:T(8,128)S(1)}, u32[]{:S(2)}, u32[]{:S(2)}) collective-permute-start(f32[16,16,128]{2,1,0:T(8,128)S(1)} %get-tuple-element.52), channel_id=1, source_target_pairs={{0,8},{8,0},{16,24},{24,16},{1,9},{9,1},{17,25},{25,17},{2,10},{10... | collective-permute-start | bytes 393224 | tf_op jit(solution)/shard_map/ppermute | solution.py:545
  27.9 8.3 %collective-permute-start.7 = (f32[16,16,128]{2,1,0:T(8,128)S(1)}, f32[16,16,128]{2,1,0:T(8,128)S(1)}, u32[]{:S(2)}, u32[]{:S(2)}) collective-permute-start(f32[16,16,128]{2,1,0:T(8,128)S(1)} %get-tuple-element.53), channel_id=1, source_target_pairs={{0,16},{8,24},{16,0},{24,8},{1,17},{9,25},{17,1},{25,9},{2,18},{10... | collective-permute-start | bytes 393224 | tf_op jit(solution)/shard_map/ppermute | solution.py:545
  29.5 6.8 %collective-permute-start.8 = (f32[16,16,128]{2,1,0:T(8,128)S(1)}, f32[16,16,128]{2,1,0:T(8,128)S(1)}, u32[]{:S(2)}, u32[]{:S(2)}) collective-permute-start(f32[16,16,128]{2,1,0:T(8,128)S(1)} %get-tuple-element.54), channel_id=1, source_target_pairs={{0,24},{8,16},{16,8},{24,0},{1,25},{9,17},{17,9},{25,1},{2,26},{10... | collective-permute-start | bytes 393224 | tf_op jit(solution)/shard_map/ppermute | solution.py:545
